TPU v7x, 256 devices: a whole 4x4x8 slice. The times are simulated.
256 devices in a mesh: seg: 32 (over x, z), tp: 8 (over y, core).
Axes of the slice: x: 4, y: 4, z: 8, core: 2. Of those that a mesh axis runs over, the one named last changes fastest.
Arguments:
- queries: bfloat16 [8192, 8192], P('seg', 'tp'), may hold values from -8 to 8
- keys_own: bfloat16 [8192, 1024], P('seg', 'tp'), may hold values from -8 to 8
- values_own: bfloat16 [8192, 1024], P('seg', 'tp'), may hold values from -6 to 6
- out_grad: bfloat16 [8192, 8192], P('seg', 'tp'), may hold values from -6 to 6
- summary_states: bfloat16 [1600, 8192], P('seg'), may hold values from -6 to 6
- w_key: bfloat16 [8192, 1024], P(None, 'tp'), may hold values from -0.0625 to 0.0625
- w_value: bfloat16 [8192, 1024], P(None, 'tp'), may hold values from -0.0625 to 0.0625
- summary_grad: bfloat16 [1600, 8192], P('seg', 'tp'), may hold values from -6 to 6
Outputs:
- query_grad: bfloat16 [8192, 8192], P('seg', 'tp')
- key_grad: bfloat16 [8192, 1024], P('seg', 'tp')
- value_grad: bfloat16 [8192, 1024], P('seg', 'tp')
- state_grad: bfloat16 [1600, 8192], P('seg', 'tp')
All inputs are finite; a program needn't handle non-finite values.
Results may differ from a plain program's by a relative error of at most 0.023.
Values may be sent and summed in bfloat16 or wider, within the bound.
A program may use at most 256 MiB of HBM per device.

v0:
```python
import jax
import jax.numpy as jnp
from jax import lax
from jax.sharding import PartitionSpec as P

HEADS = 64
KVH = 8
HD = 128


def per_device(
    queries, keys_own, values_own, out_grad, summary_states, w_key, w_value, summary_grad
):
    rows = queries.shape[0]
    kv_local = keys_own.shape[1] // HD
    group = HEADS // KVH
    scale = HD ** (-0.5)
    count = summary_states.shape[0]
    segments = lax.axis_size("seg")
    position = lax.axis_index("seg")
    nsum = count * segments
    nkeys = nsum + rows
    width = kv_local * HD
    projected = jnp.concatenate(
        [
            jnp.dot(summary_states, w_key, preferred_element_type=jnp.float32).astype(jnp.bfloat16),
            jnp.dot(summary_states, w_value, preferred_element_type=jnp.float32).astype(
                jnp.bfloat16
            ),
        ],
        axis=1,
    )
    everyone = lax.all_gather(projected, "seg", axis=0, tiled=True)
    keys_all = jnp.concatenate([everyone[:, :width], keys_own], 0)
    vals_all = jnp.concatenate([everyone[:, width:], values_own], 0)
    row_pos = jnp.arange(rows)[:, None]
    col_pos = jnp.arange(nkeys)[None, :]
    visible = jnp.where(col_pos < nsum, col_pos < position * count, col_pos - nsum <= row_pos)
    query_heads = queries.reshape(rows, kv_local * group, HD).transpose(1, 0, 2)
    grad_heads = out_grad.reshape(rows, kv_local * group, HD).transpose(1, 0, 2)
    contract_last = (((1,), (1,)), ((), ()))
    contract_first = (((0,), (0,)), ((), ()))

    def head_step(carry, inputs):
        key_acc, val_acc = carry
        query_head, grad_head = inputs
        scores = (
            lax.dot_general(query_head, keys_all, contract_last, preferred_element_type=jnp.float32)
            * scale
        )
        scores = jnp.where(visible, scores, -jnp.inf)
        probs = jnp.exp(scores - jnp.max(scores, axis=-1, keepdims=True))
        probs = probs / jnp.sum(probs, axis=-1, keepdims=True)
        probs_b = probs.astype(jnp.bfloat16)
        attn = jnp.dot(probs_b, vals_all, preferred_element_type=jnp.float32)
        delta = jnp.sum(grad_head.astype(jnp.float32) * attn, axis=-1)
        dprobs = lax.dot_general(
            grad_head, vals_all, contract_last, preferred_element_type=jnp.float32
        )
        dscores = (probs * (dprobs - delta[:, None])).astype(jnp.bfloat16)
        dquery = (jnp.dot(dscores, keys_all, preferred_element_type=jnp.float32) * scale).astype(
            jnp.bfloat16
        )
        key_acc = key_acc + lax.dot_general(
            dscores, query_head, contract_first, preferred_element_type=jnp.float32
        )
        val_acc = val_acc + lax.dot_general(
            probs_b, grad_head, contract_first, preferred_element_type=jnp.float32
        )
        return ((key_acc, val_acc), dquery)

    zeros = jnp.zeros((nkeys, HD), jnp.float32)
    (key_acc, val_acc), dquery = lax.scan(head_step, (zeros, zeros), (query_heads, grad_heads))
    key_sums = [key_acc * scale]
    value_sums = [val_acc]
    query_grad = dquery.transpose(1, 0, 2).reshape(rows, kv_local * group * HD)
    key_grad = jnp.concatenate([acc[nsum:] for acc in key_sums], 1).astype(jnp.bfloat16)
    value_grad = jnp.concatenate([acc[nsum:] for acc in value_sums], 1).astype(jnp.bfloat16)
    summary_terms = jnp.concatenate(
        [acc[:nsum] for acc in key_sums] + [acc[:nsum] for acc in value_sums], 1
    )
    emitted = lax.psum_scatter(
        summary_terms.astype(jnp.bfloat16), "seg", scatter_dimension=0, tiled=True
    )
    partial_state = lax.dot_general(
        emitted[:, :width], w_key, contract_last, preferred_element_type=jnp.float32
    )
    partial_state = partial_state + lax.dot_general(
        emitted[:, width:], w_value, contract_last, preferred_element_type=jnp.float32
    )
    shared = lax.psum_scatter(
        partial_state.astype(jnp.bfloat16), "tp", scatter_dimension=1, tiled=True
    ).astype(jnp.float32)
    state_grad = (shared + summary_grad.astype(jnp.float32)).astype(jnp.bfloat16)
    return (query_grad, key_grad, value_grad, state_grad)


def solution(mesh):
    placed = (
        P("seg", "tp"),
        P("seg", "tp"),
        P("seg", "tp"),
        P("seg", "tp"),
        P("seg", None),
        P(None, "tp"),
        P(None, "tp"),
        P("seg", "tp"),
    )
    return jax.shard_map(
        per_device,
        mesh=mesh,
        in_specs=placed,
        out_specs=(P("seg", "tp"), P("seg", "tp"), P("seg", "tp"), P("seg", "tp")),
        check_vma=False,
    )
```

profile of v0, /device:TPU:1, one launch (start us, length us, event | category | flops | bytes accessed | tf_op | source)
XLA Modules:
  0.0 368.2 jit_solution(2039793102110522160)
XLA Ops:
  7.3 2.5 convolution_convert_fusion
  10.4 42.6 %all-gather = bf16[32,50,256]{2,1,0:T(8,128)(2,1)S(1)} all-gather(bf16[1,50,256]{2,1,0:T(8,128)(2,1)S(1)} %maximum_bitcast_fusion), channel_id=1, replica_groups=mesh['seg'=32,'tp'=8] {'seg'}, dimensions={0}, use_global_device_ids=true | all-gather | bytes 844800 | tf_op jit(solution)/shard_map/all_gather | solution.py:33
  60.3 105.0 %while.15 = (s32[]{:T(128)}, f32[1856,128]{1,0:T(8,128)}, f32[1856,128]{1,0:T(8,128)}, bf16[8,256,128]{2,1,0:T(8,128)(2,1)}, bf16[8,256,128]{1,2,0:T(8,128)(2,1)...) while((s32[]{:T(128)}, f32[1856,128]{1,0:T(8,128)}, ...), condition=%wide.region_4.5_spmd.clone, body=%wide.region_0.4_spmd.clone.sunk | while | flops 738049280 | bytes 25123396 | solution.py:73
  66.9 2.6 convolution_add_fusion.5
  79.4 2.9 convolution_add_fusion.5
  83.4 2.6 convolution_add_fusion.6
  92.6 2.9 convolution_add_fusion.5
  96.6 2.6 convolution_add_fusion.6
  103.5 2.3 fusion.79
  105.8 2.9 convolution_add_fusion.5
  109.8 2.6 convolution_add_fusion.6
  116.7 2.3 fusion.79
  119.0 2.9 convolution_add_fusion.5
  123.1 2.6 convolution_add_fusion.6
  129.9 2.3 fusion.79
  132.2 2.9 convolution_add_fusion.5
  136.3 2.6 convolution_add_fusion.6
  145.5 2.9 convolution_add_fusion.5
  149.5 2.6 convolution_add_fusion.6
  158.7 2.9 convolution_add_fusion.5
  162.7 2.6 convolution_add_fusion.6
  170.2 150.9 %all-reduce.3.cloned.1.call-done = bf16[1600,256]{1,0:T(8,128)(2,1)} async-done(((bf16[1600,256]{1,0:T(8,128)(2,1)}), bf16[1600,256]{1,0:T(8,128)(2,1)}) %all-reduce.3.cloned.1.call-update) | async-done | bytes 819216
  323.3 3.0 fusion.25
  329.5 30.3 %reduce-scatter.2.cloned.1.call-done = bf16[50,1024]{1,0:T(8,128)(2,1)} async-done(((bf16[50,8192]{1,0:T(8,128)(2,1)}), bf16[50,1024]{1,0:T(8,128)(2,1)}) %reduce-scatter.2.cloned.1.call-update) | async-done | bytes 102416 | tf_op jit(solution)/shard_map/reduce_scatter | solution.py:91
  (119 shorter events, 75.5 us)
Async XLA Ops:
  7.2 2.6 copy-start
  7.2 2.7 copy-start.3
  7.2 313.9 %all-reduce.3.cloned.1.call-start = ((), (), s32[]{:S(2)}) async-start(), calls=%async_computation.2 | async-start | bytes 1638400
  54.1 5.3 %copy-start.6 = (bf16[256,128]{1,0:T(8,128)(2,1)S(1)}, bf16[256,128]{1,0:T(8,128)(2,1)}, u32[]{:S(2)}) copy-start(bf16[256,128]{1,0:T(8,128)(2,1)} %param.11) | copy-start | bytes 196612
  54.1 5.3 %copy-start.7 = (bf16[256,128]{1,0:T(8,128)(2,1)S(1)}, bf16[256,128]{1,0:T(8,128)(2,1)}, u32[]{:S(2)}) copy-start(bf16[256,128]{1,0:T(8,128)(2,1)} %param.12) | copy-start | bytes 196612
  62.3 1.0 copy-start.4
  66.9 2.6 copy-start.1
  74.8 1.0 copy-start.4
  79.4 3.0 copy-start.1
  88.0 1.0 copy-start.4
  92.6 2.9 copy-start.1
  101.2 1.0 copy-start.4
  105.8 2.9 copy-start.1
  114.4 1.0 copy-start.4
  119.0 3.0 copy-start.1
  127.7 1.0 copy-start.4
  132.2 2.9 copy-start.1
  140.9 1.0 copy-start.4
  145.4 2.9 copy-start.1
  158.7 2.9 copy-start.1
  167.9 1.1 copy-start.8
  168.9 190.9 %reduce-scatter.2.cloned.1.call-start = ((), (), s32[]{:S(2)}) async-start(), calls=%async_computation.1 | async-start | bytes 1032192 | tf_op jit(solution)/shard_map/reduce_scatter | solution.py:91
  321.1 2.2 copy-start.2
  326.3 33.5 %copy-start.5 = (bf16[50,1024]{1,0:T(8,128)(2,1)S(1)}, bf16[50,1024]{1,0:T(8,128)(2,1)}, u32[]{:S(2)}) copy-start(bf16[50,1024]{1,0:T(8,128)(2,1)} %param.17) | copy-start | bytes 307204
  (1 other events, 1.0 us)
Sparse Core Ops, SparseCore 0:
  169.0 151.9 all-reduce.2
  326.5 33.2 reduce-scatter.1
where the time goes:
time: 372 us; the launch traced here: 368 us
  waiting for transfers between devices  181 us (49%)
  matrix products  102 us (27%)
  blocking collectives  42.6 us (11%)
  local copies, waits for them, and re-layouts  16.2 us (4%)
  between operations  14.8 us (4%)
  other arithmetic  11 us (3%)
    unnamed x3, waiting for transfers between devices  151 us
    all_gather x1, blocking collectives, per_device(): everyone = lax.all_gather(projected, 'seg', axis=0, tiled=True)  42.6 us
    reduce_scatter x1, waiting for transfers between devices, per_device(): lax.psum_scatter(partial_state.astype(jnp.bfloat16), 'tp', scatter_dimens...  30.3 us
    dot_general x8, matrix products, head_step(): lax.dot_general(dscores, query_head, contract_first, preferred_element_ty...  23.2 us
    dot_general x8, matrix products, head_step(): lax.dot_general(probs_b, grad_head, contract_first, preferred_element_typ...  20.5 us
    dot_general x8, matrix products, head_step(): lax.dot_general(grad_head, vals_all, contract_last, preferred_element_typ...  18.6 us
    dot_general x8, matrix products, head_step(): lax.dot_general(query_head, keys_all, contract_last, preferred_element_ty...  13.3 us
    dot_general x8, matrix products, head_step(): attn = jnp.dot(probs_b, vals_all, preferred_element_type=jnp.float32)  9.62 us
  transfers between devices with their start and end apart: 2, of which 2 were waited for; matrix products, arithmetic and copies ran while one was open for 1% of the time, Pallas kernels for 0%

commit v1 on v0

v1 whole, which is shorter than its diff:
```python
import functools
import math

import jax
import jax.numpy as jnp
from jax import lax
from jax.experimental import pallas as pl
from jax.experimental.pallas import tpu as pltpu
from jax.sharding import PartitionSpec as P

HD = 128
HEADS = 8
TOK = 256
M = 50
MAIN = 48
REM = M - MAIN
TILE = 16
NX, NZ = 4, 8
NTP = 8
GROUP = NZ * M
REM0 = NZ * MAIN
BLOCK = MAIN + TILE
D = 8192
W2 = 2 * HD
SCALE = HD ** (-0.5)
SCALE2 = SCALE * math.log2(math.e)
NEG = -1e30
F32 = jnp.float32
BF16 = jnp.bfloat16
MESH = pl.DeviceIdType.MESH
LAST = (((1,), (1,)), ((), ()))
PLAIN = (((1,), (0,)), ((), ()))
WCHUNK = 4


def dot(a, b, dims=PLAIN):
    return lax.dot_general(a, b, dims, preferred_element_type=F32)


def seg_place():
    seg = lax.axis_index("seg")
    return seg // NZ, lax.rem(seg, NZ)


def z_peer(x, z, d):
    other = lax.rem(z + d, NZ)
    return other, x * NZ + other


def x_peer(x, z, d):
    other = lax.rem(x + d, NX)
    return other, other * NZ + z


def greet(peers):
    barrier = pltpu.get_barrier_semaphore()
    for peer in peers:
        pl.semaphore_signal(barrier, inc=1, device_id=peer, device_id_type=MESH)
    return barrier, len(peers)


def load_weights(wk_hbm, wv_hbm, w, sems):
    rows = D // WCHUNK
    copies = []
    for c in range(WCHUNK):
        part = pl.ds(c * rows, rows)
        for i, src in enumerate((wk_hbm, wv_hbm)):
            copy = pltpu.make_async_copy(
                src.at[part], w.at[part, pl.ds(i * HD, HD)], sems.at[c, i]
            )
            copy.start()
            copies.append(copy)
    return copies


def gather_kernel(
    st_hbm, wk_hbm, wv_hbm, out_ref, st, w, mine, zrecv, grp, wsem, stsem, zs, zr, xs, xr
):
    x, z = seg_place()
    peers = [{"seg": z_peer(x, z, d)[1]} for d in range(1, NZ)]
    peers += [{"seg": x_peer(x, z, d)[1]} for d in range(1, NX)]
    barrier, count = greet(peers)
    stcopy = pltpu.make_async_copy(st_hbm, st, stsem)
    stcopy.start()
    wcopies = load_weights(wk_hbm, wv_hbm, w, wsem)
    stcopy.wait()
    rows = D // WCHUNK
    total = jnp.zeros((M, W2), F32)
    for c in range(WCHUNK):
        wcopies[2 * c].wait()
        wcopies[2 * c + 1].wait()
        part = pl.ds(c * rows, rows)
        total = total + dot(st[:, part], w[part, :])
    mine[0:MAIN, :] = total[0:MAIN].astype(BF16)
    row = lax.broadcasted_iota(jnp.int32, (TILE, W2), 0)
    rem = jnp.where(
        row == REM * z,
        total[MAIN : MAIN + 1],
        jnp.where(row == REM * z + 1, total[MAIN + 1 : MAIN + 2], 0.0),
    )
    mine[MAIN:BLOCK, :] = rem.astype(BF16)
    pl.semaphore_wait(barrier, count)

    def zcopy(d, peer, slot):
        return pltpu.make_async_remote_copy(
            src_ref=mine,
            dst_ref=zrecv.at[slot],
            send_sem=zs.at[d - 1],
            recv_sem=zr.at[d - 1],
            device_id={"seg": peer},
            device_id_type=MESH,
        )

    sends = []
    for d in range(1, NZ):
        copy = zcopy(d, z_peer(x, z, d)[1], z)
        copy.start()
        sends.append(copy)
    grp[x, pl.ds(pl.multiple_of(z * MAIN, TILE), MAIN), :] = mine[0:MAIN, :]
    shared = mine[MAIN:BLOCK, :].astype(F32)
    for d in range(1, NZ):
        other, peer = z_peer(x, z, NZ - d)
        zcopy(d, peer, other).wait_recv()
        grp[x, pl.ds(pl.multiple_of(other * MAIN, TILE), MAIN), :] = zrecv[other, 0:MAIN, :]
        shared = shared + zrecv[other, MAIN:BLOCK, :].astype(F32)
    grp[x, REM0:GROUP, :] = shared.astype(BF16)

    def xcopy(d, peer, g):
        return pltpu.make_async_remote_copy(
            src_ref=grp.at[g],
            dst_ref=grp.at[g],
            send_sem=xs.at[d - 1],
            recv_sem=xr.at[d - 1],
            device_id={"seg": peer},
            device_id_type=MESH,
        )

    for d in range(1, NX):

        @pl.when(x + d < NX)
        def _(d=d):
            xcopy(d, x_peer(x, z, d)[1], x).start()

    for copy in sends:
        copy.wait_send()
    out_ref[x] = grp[x]
    for d in range(1, NX):

        @pl.when(x >= d)
        def _(d=d):
            other, peer = x_peer(x, z, NX - d)
            xcopy(d, peer, other).wait_recv()
            out_ref[other] = grp[other]

    for d in range(1, NX):

        @pl.when(x + d < NX)
        def _(d=d):
            xcopy(d, x_peer(x, z, d)[1], x).wait_send()


def gather(states, w_key, w_value):
    return pl.pallas_call(
        gather_kernel,
        name="gather",
        out_shape=jax.ShapeDtypeStruct((NX, GROUP, W2), BF16),
        in_specs=[pl.BlockSpec(memory_space=pl.ANY)] * 3,
        out_specs=pl.BlockSpec(memory_space=pltpu.VMEM),
        scratch_shapes=[
            pltpu.VMEM((M, D), BF16),
            pltpu.VMEM((D, W2), BF16),
            pltpu.VMEM((BLOCK, W2), BF16),
            pltpu.VMEM((NZ, BLOCK, W2), BF16),
            pltpu.VMEM((NX, GROUP, W2), BF16),
            pltpu.SemaphoreType.DMA((WCHUNK, 2)),
            pltpu.SemaphoreType.DMA,
            pltpu.SemaphoreType.DMA((NZ - 1,)),
            pltpu.SemaphoreType.DMA((NZ - 1,)),
            pltpu.SemaphoreType.DMA((NX - 1,)),
            pltpu.SemaphoreType.DMA((NX - 1,)),
        ],
        compiler_params=pltpu.CompilerParams(
            collective_id=0, has_side_effects=True, vmem_limit_bytes=24 << 20
        ),
    )(states, w_key, w_value)


def attention_kernel(
    q_ref, g_ref, ko_ref, vo_ref, grp_ref, dq_ref, dko_ref, dvo_ref, part_ref,
    s_own, p_own, s_all, p_all, m_ref, l_ref, d_ref, dqt, kt_own, kt, dk_acc, dv_acc,
):
    x, z = seg_place()
    groups = x + jnp.minimum(z, 1)

    def head(ref, h):
        return ref[:, pl.ds(pl.multiple_of(h * HD, HD), HD)]

    def lanes(h):
        return pl.ds(pl.multiple_of(h * TOK, TOK), TOK)

    def sweep_one(keys, vals, s_ref, p_ref, mask, first):
        def step(h, carry):
            s = dot(keys, head(q_ref, h), LAST)
            if mask is not None:
                s = jnp.where(mask, s, NEG)
            s_ref[:, lanes(h)] = s
            top = jnp.max(s, axis=0, keepdims=True)
            p = dot(vals, head(g_ref, h), LAST)
            p_ref[:, lanes(h)] = p
            if not first:
                old = m_ref[:, lanes(h)]
                top = jnp.maximum(old, top)
            e = jnp.exp2(s * SCALE2 - top * SCALE2)
            total = jnp.sum(e, axis=0, keepdims=True)
            inner = jnp.sum(e * p, axis=0, keepdims=True)
            if not first:
                fade = jnp.exp2((old - top) * SCALE2)
                total = total + l_ref[:, lanes(h)] * fade
                inner = inner + d_ref[:, lanes(h)] * fade
            m_ref[:, lanes(h)] = top
            l_ref[:, lanes(h)] = total
            d_ref[:, lanes(h)] = inner
            return carry

        lax.fori_loop(0, HEADS, step, 0)

    def sweep_two(s_ref, p_ref, keys_t, first):
        dk_acc_n = dk_acc.at[0 : s_ref.shape[0]]
        dv_acc_n = dv_acc.at[0 : s_ref.shape[0]]
        dk_acc_n[...] = jnp.zeros_like(dk_acc_n)
        dv_acc_n[...] = jnp.zeros_like(dv_acc_n)

        def step(h, carry):
            probs = jnp.exp2(s_ref[:, lanes(h)] * SCALE2 - m_ref[:, lanes(h)])
            ds = (probs * (p_ref[:, lanes(h)] - d_ref[:, lanes(h)])).astype(BF16)
            dv_acc_n[...] += dot(probs.astype(BF16), head(g_ref, h))
            dk_acc_n[...] += dot(ds, head(q_ref, h))
            update = dot(keys_t[...], ds)
            if first:
                dqt[:, lanes(h)] = update
            else:
                dqt[:, lanes(h)] += update
            return carry

        lax.fori_loop(0, HEADS, step, 0)
        return dk_acc_n[...] * SCALE, dv_acc_n[...]

    tri = lax.broadcasted_iota(jnp.int32, (TOK, TOK), 0) <= lax.broadcasted_iota(
        jnp.int32, (TOK, TOK), 1
    )
    kt_own[...] = ko_ref[...].astype(F32).T.astype(BF16)
    sweep_one(ko_ref[...], vo_ref[...], s_own, p_own, tri, True)

    def full_group(g, carry):
        sweep_one(
            grp_ref[g, :, 0:HD], grp_ref[g, :, HD:W2], s_all.at[g], p_all.at[g], None, False
        )
        return carry

    lax.fori_loop(0, x, full_group, 0)

    @pl.when(z > 0)
    def _():
        r = lax.broadcasted_iota(jnp.int32, (GROUP, TOK), 0)
        mask = (r < MAIN * z) | ((r >= REM0) & (r < REM0 + REM * z))
        sweep_one(
            grp_ref[x, :, 0:HD], grp_ref[x, :, HD:W2], s_all.at[x], p_all.at[x], mask, False
        )

    d_ref[...] = d_ref[...] / l_ref[...]
    m_ref[...] = m_ref[...] * SCALE2 + jnp.log2(l_ref[...])

    dk, dv = sweep_two(s_own, p_own, kt_own, True)
    dko_ref[...] = dk.astype(BF16)
    dvo_ref[...] = dv.astype(BF16)
    part_ref[x] = jnp.zeros((GROUP, W2), BF16)

    def back_group(g, carry):
        kt[...] = grp_ref[g, :, 0:HD].astype(F32).T.astype(BF16)
        dk, dv = sweep_two(s_all.at[g], p_all.at[g], kt, False)
        part_ref[g, :, 0:HD] = dk.astype(BF16)
        part_ref[g, :, HD:W2] = dv.astype(BF16)
        return carry

    lax.fori_loop(0, groups, back_group, 0)
    for h in range(HEADS):
        dq_ref[:, h * HD : (h + 1) * HD] = (
            (dqt[:, h * TOK : (h + 1) * TOK] * SCALE).T.astype(BF16)
        )


def attention(queries, out_grad, keys_own, values_own, grp):
    vmem = pl.BlockSpec(memory_space=pltpu.VMEM)
    rows = HEADS * TOK
    return pl.pallas_call(
        attention_kernel,
        name="attention",
        out_shape=(
            jax.ShapeDtypeStruct((TOK, HEADS * HD), BF16),
            jax.ShapeDtypeStruct((TOK, HD), BF16),
            jax.ShapeDtypeStruct((TOK, HD), BF16),
            jax.ShapeDtypeStruct((NX, GROUP, W2), BF16),
        ),
        in_specs=[vmem] * 5,
        out_specs=(vmem,) * 4,
        scratch_shapes=[
            pltpu.VMEM((TOK, rows), F32),
            pltpu.VMEM((TOK, rows), F32),
            pltpu.VMEM((NX, GROUP, rows), F32),
            pltpu.VMEM((NX, GROUP, rows), F32),
            pltpu.VMEM((1, rows), F32),
            pltpu.VMEM((1, rows), F32),
            pltpu.VMEM((1, rows), F32),
            pltpu.VMEM((HD, rows), F32),
            pltpu.VMEM((HD, TOK), BF16),
            pltpu.VMEM((HD, GROUP), BF16),
            pltpu.VMEM((GROUP, HD), F32),
            pltpu.VMEM((GROUP, HD), F32),
        ],
        compiler_params=pltpu.CompilerParams(vmem_limit_bytes=56 << 20),
    )(queries, out_grad, keys_own, values_own, grp)


def scatter_kernel(
    part_ref, wk_hbm, wv_hbm, sg_ref, out_ref,
    w, xrecv, zsend, zrecv, em, tsend, trecv, wsem, xs, xr, zs, zr, ts, tr,
):
    x, z = seg_place()
    tp = lax.axis_index("tp")
    peers = [{"seg": z_peer(x, z, d)[1]} for d in range(1, NZ)]
    peers += [{"seg": x_peer(x, z, d)[1]} for d in range(1, NX)]
    peers += [{"tp": lax.rem(tp + d, NTP)} for d in range(1, NTP)]
    barrier, count = greet(peers)
    wcopies = load_weights(wk_hbm, wv_hbm, w, wsem)
    pl.semaphore_wait(barrier, count)

    def xcopy(d, peer, g, slot):
        return pltpu.make_async_remote_copy(
            src_ref=part_ref.at[g],
            dst_ref=xrecv.at[slot],
            send_sem=xs.at[d - 1],
            recv_sem=xr.at[d - 1],
            device_id={"seg": peer},
            device_id_type=MESH,
        )

    for d in range(1, NX):

        @pl.when(x >= d)
        def _(d=d):
            other, peer = x_peer(x, z, NX - d)
            xcopy(d, peer, other, d - 1).start()

    xrecv[NX - 1] = part_ref[x]
    for d in range(1, NX):

        @pl.when(x + d < NX)
        def _(d=d):
            other, peer = x_peer(x, z, d)
            xcopy(d, peer, other, d - 1).wait_recv()
            xrecv[NX - 1] = (xrecv[NX - 1].astype(F32) + xrecv[d - 1].astype(F32)).astype(BF16)

    for i in range(NZ):
        zsend[i, 0:MAIN, :] = xrecv[NX - 1, i * MAIN : (i + 1) * MAIN, :]
        zsend[i, MAIN:BLOCK, :] = xrecv[NX - 1, REM0:GROUP, :]

    def zcopy(d, other, peer):
        return pltpu.make_async_remote_copy(
            src_ref=zsend.at[other],
            dst_ref=zrecv.at[d - 1],
            send_sem=zs.at[d - 1],
            recv_sem=zr.at[d - 1],
            device_id={"seg": peer},
            device_id_type=MESH,
        )

    for d in range(1, NZ):
        zcopy(d, *z_peer(x, z, d)).start()
    total = zsend[z].astype(F32)
    for d in range(1, NZ):
        zcopy(d, *z_peer(x, z, NZ - d)).wait_recv()
        total = total + zrecv[d - 1].astype(F32)
    row = lax.broadcasted_iota(jnp.int32, (TILE, W2), 0)
    rem = total[MAIN:BLOCK]
    one = jnp.sum(jnp.where(row == REM * z, rem, 0.0), axis=0, keepdims=True)
    two = jnp.sum(jnp.where(row == REM * z + 1, rem, 0.0), axis=0, keepdims=True)
    em[0:MAIN, :] = total[0:MAIN].astype(BF16)
    em[MAIN:BLOCK, :] = jnp.where(row == 0, one, jnp.where(row == 1, two, 0.0)).astype(BF16)
    for copy in wcopies:
        copy.wait()
    cols = D // NTP

    def state(target):
        part = pl.ds(pl.multiple_of(target * cols, cols), cols)
        return dot(em[...], w[part, :], LAST)[0:M]

    def tcopy(d, target):
        return pltpu.make_async_remote_copy(
            src_ref=tsend.at[d - 1],
            dst_ref=trecv.at[d - 1],
            send_sem=ts.at[d - 1],
            recv_sem=tr.at[d - 1],
            device_id={"tp": target},
            device_id_type=MESH,
        )

    def send_state(d):
        target = lax.rem(tp + d, NTP)
        tsend[d - 1] = state(target).astype(BF16)
        tcopy(d, target).start()

    for d in range(1, NTP):
        send_state(d)
    out = state(tp) + sg_ref[...].astype(F32)
    for d in range(1, NTP):
        tcopy(d, lax.rem(tp + NTP - d, NTP)).wait_recv()
        out = out + trecv[d - 1].astype(F32)
    out_ref[...] = out.astype(BF16)
    for d in range(1, NX):

        @pl.when(x >= d)
        def _(d=d):
            other, peer = x_peer(x, z, NX - d)
            xcopy(d, peer, other, d - 1).wait_send()

    for d in range(1, NZ):
        zcopy(d, *z_peer(x, z, d)).wait_send()
    for d in range(1, NTP):
        tcopy(d, lax.rem(tp + d, NTP)).wait_send()


def scatter(part, w_key, w_value, summary_grad):
    vmem = pl.BlockSpec(memory_space=pltpu.VMEM)
    anywhere = pl.BlockSpec(memory_space=pl.ANY)
    cols = D // NTP
    return pl.pallas_call(
        scatter_kernel,
        name="scatter",
        out_shape=jax.ShapeDtypeStruct((M, cols), BF16),
        in_specs=[vmem, anywhere, anywhere, vmem],
        out_specs=vmem,
        scratch_shapes=[
            pltpu.VMEM((D, W2), BF16),
            pltpu.VMEM((NX, GROUP, W2), BF16),
            pltpu.VMEM((NZ, BLOCK, W2), BF16),
            pltpu.VMEM((NZ - 1, BLOCK, W2), BF16),
            pltpu.VMEM((BLOCK, W2), BF16),
            pltpu.VMEM((NTP - 1, M, cols), BF16),
            pltpu.VMEM((NTP - 1, M, cols), BF16),
            pltpu.SemaphoreType.DMA((WCHUNK, 2)),
            pltpu.SemaphoreType.DMA((NX - 1,)),
            pltpu.SemaphoreType.DMA((NX - 1,)),
            pltpu.SemaphoreType.DMA((NZ - 1,)),
            pltpu.SemaphoreType.DMA((NZ - 1,)),
            pltpu.SemaphoreType.DMA((NTP - 1,)),
            pltpu.SemaphoreType.DMA((NTP - 1,)),
        ],
        compiler_params=pltpu.CompilerParams(
            collective_id=1, has_side_effects=True, vmem_limit_bytes=24 << 20
        ),
    )(part, w_key, w_value, summary_grad)


def per_device(
    queries, keys_own, values_own, out_grad, summary_states, w_key, w_value, summary_grad
):
    grp = gather(summary_states, w_key, w_value)
    query_grad, key_grad, value_grad, part = attention(
        queries, out_grad, keys_own, values_own, grp
    )
    state_grad = scatter(part, w_key, w_value, summary_grad)
    return (query_grad, key_grad, value_grad, state_grad)


def solution(mesh):
    placed = (
        P("seg", "tp"),
        P("seg", "tp"),
        P("seg", "tp"),
        P("seg", "tp"),
        P("seg", None),
        P(None, "tp"),
        P(None, "tp"),
        P("seg", "tp"),
    )
    return jax.shard_map(
        per_device,
        mesh=mesh,
        in_specs=placed,
        out_specs=(P("seg", "tp"), P("seg", "tp"), P("seg", "tp"), P("seg", "tp")),
        check_vma=False,
    )
```

time: 372 us -> 98.4 us (0.26)
  waiting for transfers between devices: 181 us -> 0 us
  matrix products: 102 us -> 0 us
  Pallas kernels: 0 us -> 90.5 us
  blocking collectives: 42.6 us -> 0 us
  between operations: 14.8 us -> 0.69 us
  other arithmetic: 11 us -> 0 us
  local copies, waits for them, and re-layouts: 16.2 us -> 7.03 us
    unnamed x3 -> x0, waiting for transfers between devices: 151 us -> none
    dot_general x52 -> x0, matrix products: 102 us -> none  [the longest x8 23.2 us: head_step(): lax.dot_general(dscores, query_head, contract_first, preferred_element_ty...]
    pallas_call x0 -> x3, Pallas kernels: none -> 90.5 us  [the longest x1 60.3 us: scatter(): pl.pallas_call(scatter_kernel, name='scatter', out_shape=jax.ShapeDtypeSt...]
    all_gather x1 -> x0, blocking collectives: 42.6 us -> none  [per_device(): everyone = lax.all_gather(projected, 'seg', axis=0, tiled=True)]
    reduce_scatter x1 -> x0, waiting for transfers between devices: 30.3 us -> none  [per_device(): lax.psum_scatter(partial_state.astype(jnp.bfloat16), 'tp', scatter_dimens...]
    while x32 -> x0, local copies, waits for them, and re-layouts: 5.82 us -> none
    convert_element_type x9 -> x0, other arithmetic: 3.96 us -> none  [the longest x8 2.38 us: head_step(): probs_b = probs.astype(jnp.bfloat16)]
  transfers between devices with their start and end apart: 2 -> 0, of which waited for: 2 -> 0; matrix products, arithmetic and copies ran while one was open for 1% -> 0% of each run, Pallas kernels for 0% -> 0%
where the time goes in v1:
time: 98.4 us; the launch traced here: 98.2 us
  Pallas kernels  90.5 us (92%)
  local copies, waits for them, and re-layouts  7.03 us (7%)
    pallas_call x1, Pallas kernels, scatter(): pl.pallas_call(scatter_kernel, name='scatter', out_shape=jax.ShapeDtypeSt...  60.3 us
    pallas_call x1, Pallas kernels, gather(): pl.pallas_call(gather_kernel, name='gather', out_shape=jax.ShapeDtypeStru...  22.9 us
    pallas_call x1, Pallas kernels, attention(): pl.pallas_call(attention_kernel, name='attention', out_shape=(jax.ShapeDt...  7.26 us
    unnamed x17, local copies, waits for them, and re-layouts  7.03 us

profile of v1, /device:TPU:1, one launch (start us, length us, event | category | flops | bytes accessed | tf_op | source)
XLA Modules:
  0.0 98.2 jit_solution(2396564579627047050)
XLA Ops:
  0.6 0.0 copy-start
  0.6 1.6 %copy-done = bf16[8192,128]{1,0:T(8,128)(2,1)S(1)} copy-done((bf16[8192,128]{1,0:T(8,128)(2,1)S(1)}, bf16[8192,128]{1,0:T(8,128)(2,1)}, u32[]{:S(2)}) %copy-start) | copy-done | bytes 2097176
  2.2 0.0 copy-start.2
  2.2 1.6 %copy-done.2 = bf16[8192,128]{1,0:T(8,128)(2,1)S(1)} copy-done((bf16[8192,128]{1,0:T(8,128)(2,1)S(1)}, bf16[8192,128]{1,0:T(8,128)(2,1)}, u32[]{:S(2)}) %copy-start.2) | copy-done | bytes 2097176
  3.8 0.0 copy-start.5
  3.8 1.2 %copy-done.5 = bf16[50,8192]{1,0:T(8,128)(2,1)S(1)} copy-done((bf16[50,8192]{1,0:T(8,128)(2,1)S(1)}, bf16[50,8192]{1,0:T(8,128)(2,1)}, u32[]{:S(2)}) %copy-start.5) | copy-done | bytes 819224
  5.0 0.0 copy-start.1
  5.0 0.0 copy-start.3
  5.0 0.0 copy-start.7
  5.0 22.9 %gather.1.grp_ref = bf16[4,400,256]{2,1,0:T(8,128)(2,1)S(1)} custom-call(bf16[50,8192]{1,0:T(8,128)(2,1)S(1)} %copy-done.5, bf16[8192,128]{1,0:T(8,128)(2,1)S(1)} %copy-done, bf16[8192,128]{1,0:T(8,128)(2,1)S(1)} %copy-done.2), custom_call_target="tpu_custom_call" | custom-call | tf_op jit(solution)/shard_map/gather/pallas_call | solution.py:163
  27.9 0.0 copy-start.4
  27.9 0.9 copy-done.4
  28.8 7.3 %attention.1 = (bf16[256,1024]{1,0:T(8,128)(2,1)}, bf16[256,128]{1,0:T(8,128)(2,1)}, bf16[256,128]{1,0:T(8,128)(2,1)}, bf16[4,400,256]{2,1,0:T(8,128)(2,1)}) custom-call(bf16[256,1024]{1,0:T(8,128)(2,1)} %q_ref.1, bf16[256,1024]{1,0:T(8,128)(2,1)} %g_ref.1, bf16[256,128]{1,0:T(8,128)(2,1)} %ko_ref.1, bf16[256,128]{1,0:T(8,128)(2,1)} %vo_ref.1, ...), custom_call_target="tpu_custom_call" | custom-call | tf_op jit(solution)/shard_map/attention/pallas_call | solution.py:295
  36.1 0.0 copy-done.1
  36.1 0.0 copy-done.3
  36.1 0.0 copy-done.7
  36.1 0.0 copy-start.6
  36.1 1.1 %copy-done.6 = bf16[4,400,256]{2,1,0:T(8,128)(2,1)S(1)} copy-done((bf16[4,400,256]{2,1,0:T(8,128)(2,1)S(1)}, bf16[4,400,256]{2,1,0:T(8,128)(2,1)}, u32[]{:S(2)}) %copy-start.6) | copy-done | bytes 819224
  37.2 60.3 %scatter.1 = bf16[50,1024]{1,0:T(8,128)(2,1)S(1)} custom-call(bf16[4,400,256]{2,1,0:T(8,128)(2,1)S(1)} %copy-done.6, bf16[8192,128]{1,0:T(8,128)(2,1)S(1)} %copy-done.1, bf16[8192,128]{1,0:T(8,128)(2,1)S(1)} %copy-done.3, bf16[50,1024]{1,0:T(8,128)(2,1)S(1)} %copy-done.7), custom_call_target="tpu_custom_call" | custom-call | tf_op jit(solution)/shard_map/scatter/pallas_call | solution.py:436
  97.5 0.6 copy.13
Async XLA Ops:
  0.6 1.6 %copy-start = (bf16[8192,128]{1,0:T(8,128)(2,1)S(1)}, bf16[8192,128]{1,0:T(8,128)(2,1)}, u32[]{:S(2)}) copy-start(bf16[8192,128]{1,0:T(8,128)(2,1)} %wk_hbm.3) | copy-start | bytes 6291460
  2.2 1.6 %copy-start.2 = (bf16[8192,128]{1,0:T(8,128)(2,1)S(1)}, bf16[8192,128]{1,0:T(8,128)(2,1)}, u32[]{:S(2)}) copy-start(bf16[8192,128]{1,0:T(8,128)(2,1)} %wv_hbm.3) | copy-start | bytes 6291460
  3.8 1.2 %copy-start.5 = (bf16[50,8192]{1,0:T(8,128)(2,1)S(1)}, bf16[50,8192]{1,0:T(8,128)(2,1)}, u32[]{:S(2)}) copy-start(bf16[50,8192]{1,0:T(8,128)(2,1)} %st_hbm.1) | copy-start | bytes 2457604
  5.0 31.1 %copy-start.1 = (bf16[8192,128]{1,0:T(8,128)(2,1)S(1)}, bf16[8192,128]{1,0:T(8,128)(2,1)}, u32[]{:S(2)}) copy-start(bf16[8192,128]{1,0:T(8,128)(2,1)} %wk_hbm.3) | copy-start | bytes 6291460
  5.0 31.1 %copy-start.3 = (bf16[8192,128]{1,0:T(8,128)(2,1)S(1)}, bf16[8192,128]{1,0:T(8,128)(2,1)}, u32[]{:S(2)}) copy-start(bf16[8192,128]{1,0:T(8,128)(2,1)} %wv_hbm.3) | copy-start | bytes 6291460
  5.0 31.1 %copy-start.7 = (bf16[50,1024]{1,0:T(8,128)(2,1)S(1)}, bf16[50,1024]{1,0:T(8,128)(2,1)}, u32[]{:S(2)}) copy-start(bf16[50,1024]{1,0:T(8,128)(2,1)} %sg_ref.1) | copy-start | bytes 307204
  27.9 0.9 copy-start.4
  36.1 1.1 %copy-start.6 = (bf16[4,400,256]{2,1,0:T(8,128)(2,1)S(1)}, bf16[4,400,256]{2,1,0:T(8,128)(2,1)}, u32[]{:S(2)}) copy-start(bf16[4,400,256]{2,1,0:T(8,128)(2,1)} %get-tuple-element.11.part_ref) | copy-start | bytes 2457604

commit v2 on v0

v2 whole, which is shorter than its diff:
```python
import math

import jax
import jax.numpy as jnp
from jax import lax
from jax.experimental import pallas as pl
from jax.experimental.pallas import tpu as pltpu
from jax.sharding import PartitionSpec as P

HD = 128
HEADS = 8
TOK = 256
M = 50
MAIN = 48
REM = M - MAIN
TILE = 16
NX, NZ = 4, 8
NTP = 8
GROUP = NZ * M
REM0 = NZ * MAIN
BLOCK = MAIN + TILE
D = 8192
W2 = 2 * HD
SCALE = HD ** (-0.5)
SCALE2 = SCALE * math.log2(math.e)
NEG = -1e30
F32 = jnp.float32
BF16 = jnp.bfloat16
MESH = pl.DeviceIdType.MESH
LAST = (((1,), (1,)), ((), ()))
PLAIN = (((1,), (0,)), ((), ()))
WCHUNK = 4


def dot(a, b, dims=PLAIN):
    return lax.dot_general(a, b, dims, preferred_element_type=F32)


def seg_place():
    seg = lax.axis_index("seg")
    return seg // NZ, lax.rem(seg, NZ)


def z_peer(x, z, d):
    other = lax.rem(z + d, NZ)
    return other, x * NZ + other


def x_peer(x, z, d):
    other = lax.rem(x + d, NX)
    return other, other * NZ + z


def greet(peers):
    barrier = pltpu.get_barrier_semaphore()
    for peer in peers:
        pl.semaphore_signal(barrier, inc=1, device_id=peer, device_id_type=MESH)
    return barrier, len(peers)


def load_weights(wk_hbm, wv_hbm, w, sems):
    rows = D // WCHUNK
    copies = []
    for c in range(WCHUNK):
        part = pl.ds(c * rows, rows)
        for i, src in enumerate((wk_hbm, wv_hbm)):
            copy = pltpu.make_async_copy(
                src.at[part], w.at[part, pl.ds(i * HD, HD)], sems.at[c, i]
            )
            copy.start()
            copies.append(copy)
    return copies


def layer_kernel(
    q_hbm, g_hbm, ko_hbm, vo_hbm, st_hbm, wk_hbm, wv_hbm, sg_hbm,
    dq_hbm, dko_hbm, dvo_hbm, out_ref,
    q_ref, g_ref, ko_ref, vo_ref, st, w, sg_ref,
    mine, zrecv, grp, s_own, p_own, s_all, p_all, m_ref, l_ref, d_ref, dqt, kt_own, kt,
    dk_acc, dv_acc, part, xback, acc, zsend, zback, em, tsend, trecv, dq_ref, dko_ref, dvo_ref,
    wsem, insem, outsem, zs, zr, xs, xr, xbs, xbr, zbs, zbr, ts, tr,
):
    x, z = seg_place()
    tp = lax.axis_index("tp")
    peers = [{"seg": z_peer(x, z, d)[1]} for d in range(1, NZ)]
    peers += [{"seg": x_peer(x, z, d)[1]} for d in range(1, NX)]
    peers += [{"tp": lax.rem(tp + d, NTP)} for d in range(1, NTP)]
    barrier, count = greet(peers)

    loads = []
    for i, (src, dst) in enumerate(
        (
            (st_hbm, st),
            (q_hbm, q_ref),
            (ko_hbm, ko_ref),
            (g_hbm, g_ref),
            (vo_hbm, vo_ref),
            (sg_hbm, sg_ref),
        )
    ):
        loads.append(pltpu.make_async_copy(src, dst, insem.at[i]))
    loads[0].start()
    wcopies = load_weights(wk_hbm, wv_hbm, w, wsem)
    for copy in loads[1:]:
        copy.start()

    loads[0].wait()
    rows = D // WCHUNK
    total = jnp.zeros((M, W2), F32)
    for c in range(WCHUNK):
        wcopies[2 * c].wait()
        wcopies[2 * c + 1].wait()
        chunk = pl.ds(c * rows, rows)
        total = total + dot(st[:, chunk], w[chunk, :])
    mine[0:MAIN, :] = total[0:MAIN].astype(BF16)
    row = lax.broadcasted_iota(jnp.int32, (TILE, W2), 0)
    shared = jnp.where(
        row == REM * z,
        total[MAIN : MAIN + 1],
        jnp.where(row == REM * z + 1, total[MAIN + 1 : MAIN + 2], 0.0),
    )
    mine[MAIN:BLOCK, :] = shared.astype(BF16)
    pl.semaphore_wait(barrier, count)

    def zcopy(d, peer, slot):
        return pltpu.make_async_remote_copy(
            src_ref=mine,
            dst_ref=zrecv.at[slot],
            send_sem=zs.at[d - 1],
            recv_sem=zr.at[d - 1],
            device_id={"seg": peer},
            device_id_type=MESH,
        )

    for d in range(1, NZ):
        zcopy(d, z_peer(x, z, d)[1], z).start()

    def head(ref, h):
        return ref[:, h * HD : (h + 1) * HD]

    def lanes(h):
        return slice(h * TOK, (h + 1) * TOK)

    def sweep_one(keys, vals, s_ref, p_ref, mask, first):
        for h in range(HEADS):
            s = dot(keys, head(q_ref, h), LAST)
            if mask is not None:
                s = jnp.where(mask, s, NEG)
            s_ref[:, lanes(h)] = s
            top = jnp.max(s, axis=0, keepdims=True)
            p = dot(vals, head(g_ref, h), LAST)
            p_ref[:, lanes(h)] = p
            if not first:
                old = m_ref[:, lanes(h)]
                top = jnp.maximum(old, top)
            e = jnp.exp2(s * SCALE2 - top * SCALE2)
            total = jnp.sum(e, axis=0, keepdims=True)
            inner = jnp.sum(e * p, axis=0, keepdims=True)
            if not first:
                fade = jnp.exp2((old - top) * SCALE2)
                total = total + l_ref[:, lanes(h)] * fade
                inner = inner + d_ref[:, lanes(h)] * fade
            m_ref[:, lanes(h)] = top
            l_ref[:, lanes(h)] = total
            d_ref[:, lanes(h)] = inner

    def sweep_two(s_ref, p_ref, keys_t):
        count = s_ref.shape[0]
        dk = dk_acc.at[0:count]
        dv = dv_acc.at[0:count]
        for h in range(HEADS):
            probs = jnp.exp2(s_ref[:, lanes(h)] * SCALE2 - m_ref[:, lanes(h)])
            ds = (probs * (p_ref[:, lanes(h)] - d_ref[:, lanes(h)])).astype(BF16)
            dv_new = dot(probs.astype(BF16), head(g_ref, h))
            dk_new = dot(ds, head(q_ref, h))
            if h:
                dv[...] += dv_new
                dk[...] += dk_new
            else:
                dv[...] = dv_new
                dk[...] = dk_new
            dqt[:, lanes(h)] += dot(keys_t[...], ds)
        return dk[...] * SCALE, dv[...]

    tri = lax.broadcasted_iota(jnp.int32, (TOK, TOK), 0) <= lax.broadcasted_iota(
        jnp.int32, (TOK, TOK), 1
    )
    for copy in loads[1:]:
        copy.wait()
    kt_own[...] = ko_ref[...].astype(F32).T.astype(BF16)
    dqt[...] = jnp.zeros_like(dqt)
    sweep_one(ko_ref[...], vo_ref[...], s_own, p_own, tri, True)

    grp[x, pl.ds(pl.multiple_of(z * MAIN, TILE), MAIN), :] = mine[0:MAIN, :]
    shared = mine[MAIN:BLOCK, :].astype(F32)
    for d in range(1, NZ):
        other, peer = z_peer(x, z, NZ - d)
        zcopy(d, peer, other).wait_recv()
        grp[x, pl.ds(pl.multiple_of(other * MAIN, TILE), MAIN), :] = zrecv[other, 0:MAIN, :]
        shared = shared + zrecv[other, MAIN:BLOCK, :].astype(F32)
    grp[x, REM0:GROUP, :] = shared.astype(BF16)

    def xcopy(d, g):
        other = lax.rem(x + d + NX, NX)
        return pltpu.make_async_remote_copy(
            src_ref=grp.at[g],
            dst_ref=grp.at[g],
            send_sem=xs.at[jnp.abs(d) - 1],
            recv_sem=xr.at[jnp.abs(d) - 1],
            device_id={"seg": other * NZ + z},
            device_id_type=MESH,
        )

    lax.fori_loop(1, NX - x, lambda d, c: (xcopy(d, x).start(), c)[1], 0)

    @pl.when(z > 0)
    def _():
        r = lax.broadcasted_iota(jnp.int32, (GROUP, TOK), 0)
        mask = (r < MAIN * z) | ((r >= REM0) & (r < REM0 + REM * z))
        sweep_one(grp[x, :, 0:HD], grp[x, :, HD:W2], s_all.at[x], p_all.at[x], mask, False)

    def full_group(d, carry):
        g = x - d
        xcopy(-d, g).wait_recv()
        sweep_one(grp[g, :, 0:HD], grp[g, :, HD:W2], s_all.at[g], p_all.at[g], None, False)
        return carry

    lax.fori_loop(1, x + 1, full_group, 0)
    d_ref[...] = d_ref[...] / l_ref[...]
    m_ref[...] = m_ref[...] * SCALE2 + jnp.log2(l_ref[...])

    def xback_copy(d, g):
        other = lax.rem(x + d + NX, NX)
        slot = jnp.abs(d) - 1
        return pltpu.make_async_remote_copy(
            src_ref=part.at[g],
            dst_ref=xback.at[slot],
            send_sem=xbs.at[slot],
            recv_sem=xbr.at[slot],
            device_id={"seg": other * NZ + z},
            device_id_type=MESH,
        )

    acc[...] = jnp.zeros_like(acc)

    def back_group(g, carry):
        kt[...] = grp[g, :, 0:HD].astype(F32).T.astype(BF16)
        dk, dv = sweep_two(s_all.at[g], p_all.at[g], kt)

        @pl.when(g < x)
        def _():
            part[g, :, 0:HD] = dk.astype(BF16)
            part[g, :, HD:W2] = dv.astype(BF16)
            xback_copy(g - x, g).start()

        @pl.when(g == x)
        def _():
            acc[:, 0:HD] = dk
            acc[:, HD:W2] = dv

        return carry

    lax.fori_loop(0, x + jnp.minimum(z, 1), back_group, 0)

    def add_group(d, carry):
        xback_copy(d, x).wait_recv()
        acc[...] += xback[d - 1].astype(F32)
        return carry

    lax.fori_loop(1, NX - x, add_group, 0)

    for i in range(NZ):
        zsend[i, 0:MAIN, :] = acc[i * MAIN : (i + 1) * MAIN, :].astype(BF16)
        zsend[i, MAIN:BLOCK, :] = acc[REM0:GROUP, :].astype(BF16)

    def zback_copy(d, other, peer):
        return pltpu.make_async_remote_copy(
            src_ref=zsend.at[other],
            dst_ref=zback.at[d - 1],
            send_sem=zbs.at[d - 1],
            recv_sem=zbr.at[d - 1],
            device_id={"seg": peer},
            device_id_type=MESH,
        )

    for d in range(1, NZ):
        zback_copy(d, *z_peer(x, z, d)).start()

    dk, dv = sweep_two(s_own, p_own, kt_own)
    dko_ref[...] = dk.astype(BF16)
    dvo_ref[...] = dv.astype(BF16)
    for h in range(HEADS):
        dq_ref[:, h * HD : (h + 1) * HD] = (dqt[:, lanes(h)] * SCALE).T.astype(BF16)
    stores = [
        pltpu.make_async_copy(src, dst, outsem.at[i])
        for i, (src, dst) in enumerate(((dq_ref, dq_hbm), (dko_ref, dko_hbm), (dvo_ref, dvo_hbm)))
    ]
    for copy in stores:
        copy.start()

    total = zsend[z].astype(F32)
    for d in range(1, NZ):
        zback_copy(d, *z_peer(x, z, NZ - d)).wait_recv()
        total = total + zback[d - 1].astype(F32)
    rem = total[MAIN:BLOCK]
    one = jnp.sum(jnp.where(row == REM * z, rem, 0.0), axis=0, keepdims=True)
    two = jnp.sum(jnp.where(row == REM * z + 1, rem, 0.0), axis=0, keepdims=True)
    em[0:MAIN, :] = total[0:MAIN].astype(BF16)
    em[MAIN:BLOCK, :] = jnp.where(row == 0, one, jnp.where(row == 1, two, 0.0)).astype(BF16)

    cols = D // NTP

    def state(target):
        chunk = pl.ds(pl.multiple_of(target * cols, cols), cols)
        return dot(em[...], w[chunk, :], LAST)[0:M]

    def tcopy(d, target):
        return pltpu.make_async_remote_copy(
            src_ref=tsend.at[d - 1],
            dst_ref=trecv.at[d - 1],
            send_sem=ts.at[d - 1],
            recv_sem=tr.at[d - 1],
            device_id={"tp": target},
            device_id_type=MESH,
        )

    for d in range(1, NTP):
        target = lax.rem(tp + d, NTP)
        tsend[d - 1] = state(target).astype(BF16)
        tcopy(d, target).start()
    out = state(tp) + sg_ref[...].astype(F32)
    for d in range(1, NTP):
        tcopy(d, lax.rem(tp + NTP - d, NTP)).wait_recv()
        out = out + trecv[d - 1].astype(F32)
    out_ref[...] = out.astype(BF16)

    for copy in stores:
        copy.wait()
    for d in range(1, NZ):
        other, peer = z_peer(x, z, d)
        zcopy(d, peer, z).wait_send()
        zback_copy(d, other, peer).wait_send()
    lax.fori_loop(1, NX - x, lambda d, c: (xcopy(d, x).wait_send(), c)[1], 0)
    lax.fori_loop(1, x + 1, lambda d, c: (xback_copy(-d, x - d).wait_send(), c)[1], 0)
    for d in range(1, NTP):
        tcopy(d, lax.rem(tp + d, NTP)).wait_send()


def per_device(
    queries, keys_own, values_own, out_grad, summary_states, w_key, w_value, summary_grad
):
    anywhere = pl.BlockSpec(memory_space=pl.ANY)
    rows = HEADS * TOK
    cols = D // NTP
    dma = pltpu.SemaphoreType.DMA
    return pl.pallas_call(
        layer_kernel,
        name="layer",
        out_shape=(
            jax.ShapeDtypeStruct((TOK, HEADS * HD), BF16),
            jax.ShapeDtypeStruct((TOK, HD), BF16),
            jax.ShapeDtypeStruct((TOK, HD), BF16),
            jax.ShapeDtypeStruct((M, cols), BF16),
        ),
        in_specs=[anywhere] * 8,
        out_specs=(anywhere,) * 3 + (pl.BlockSpec(memory_space=pltpu.VMEM),),
        scratch_shapes=[
            pltpu.VMEM((TOK, HEADS * HD), BF16),
            pltpu.VMEM((TOK, HEADS * HD), BF16),
            pltpu.VMEM((TOK, HD), BF16),
            pltpu.VMEM((TOK, HD), BF16),
            pltpu.VMEM((M, D), BF16),
            pltpu.VMEM((D, W2), BF16),
            pltpu.VMEM((M, cols), BF16),
            pltpu.VMEM((BLOCK, W2), BF16),
            pltpu.VMEM((NZ, BLOCK, W2), BF16),
            pltpu.VMEM((NX, GROUP, W2), BF16),
            pltpu.VMEM((TOK, rows), F32),
            pltpu.VMEM((TOK, rows), F32),
            pltpu.VMEM((NX, GROUP, rows), F32),
            pltpu.VMEM((NX, GROUP, rows), F32),
            pltpu.VMEM((1, rows), F32),
            pltpu.VMEM((1, rows), F32),
            pltpu.VMEM((1, rows), F32),
            pltpu.VMEM((HD, rows), F32),
            pltpu.VMEM((HD, TOK), BF16),
            pltpu.VMEM((HD, GROUP), BF16),
            pltpu.VMEM((GROUP, HD), F32),
            pltpu.VMEM((GROUP, HD), F32),
            pltpu.VMEM((NX, GROUP, W2), BF16),
            pltpu.VMEM((NX - 1, GROUP, W2), BF16),
            pltpu.VMEM((GROUP, W2), F32),
            pltpu.VMEM((NZ, BLOCK, W2), BF16),
            pltpu.VMEM((NZ - 1, BLOCK, W2), BF16),
            pltpu.VMEM((BLOCK, W2), BF16),
            pltpu.VMEM((NTP - 1, M, cols), BF16),
            pltpu.VMEM((NTP - 1, M, cols), BF16),
            pltpu.VMEM((TOK, HEADS * HD), BF16),
            pltpu.VMEM((TOK, HD), BF16),
            pltpu.VMEM((TOK, HD), BF16),
            dma((WCHUNK, 2)),
            dma((6,)),
            dma((3,)),
            dma((NZ - 1,)),
            dma((NZ - 1,)),
            dma((NX - 1,)),
            dma((NX - 1,)),
            dma((NX - 1,)),
            dma((NX - 1,)),
            dma((NZ - 1,)),
            dma((NZ - 1,)),
            dma((NTP - 1,)),
            dma((NTP - 1,)),
        ],
        compiler_params=pltpu.CompilerParams(
            collective_id=0, has_side_effects=True, vmem_limit_bytes=58 << 20
        ),
    )(
        queries, out_grad, keys_own, values_own, summary_states, w_key, w_value, summary_grad
    )


def solution(mesh):
    placed = (
        P("seg", "tp"),
        P("seg", "tp"),
        P("seg", "tp"),
        P("seg", "tp"),
        P("seg", None),
        P(None, "tp"),
        P(None, "tp"),
        P("seg", "tp"),
    )
    return jax.shard_map(
        per_device,
        mesh=mesh,
        in_specs=placed,
        out_specs=(P("seg", "tp"), P("seg", "tp"), P("seg", "tp"), P("seg", "tp")),
        check_vma=False,
    )
```

time: 372 us -> 68.8 us (0.18)
  waiting for transfers between devices: 181 us -> 0 us
  matrix products: 102 us -> 0 us
  Pallas kernels: 0 us -> 61.5 us
  blocking collectives: 42.6 us -> 0 us
  between operations: 14.8 us -> 0.64 us
  other arithmetic: 11 us -> 0 us
  local copies, waits for them, and re-layouts: 16.2 us -> 6.36 us
    unnamed x3 -> x0, waiting for transfers between devices: 151 us -> none
    dot_general x52 -> x0, matrix products: 102 us -> none  [the longest x8 23.2 us: head_step(): lax.dot_general(dscores, query_head, contract_first, preferred_element_ty...]
    pallas_call x0 -> x1, Pallas kernels: none -> 61.5 us  [per_device(): pl.pallas_call(layer_kernel, name='layer', out_shape=(jax.ShapeDtypeStruc...]
    all_gather x1 -> x0, blocking collectives: 42.6 us -> none  [per_device(): everyone = lax.all_gather(projected, 'seg', axis=0, tiled=True)]
    reduce_scatter x1 -> x0, waiting for transfers between devices: 30.3 us -> none  [per_device(): lax.psum_scatter(partial_state.astype(jnp.bfloat16), 'tp', scatter_dimens...]
    while x32 -> x0, local copies, waits for them, and re-layouts: 5.82 us -> none
    convert_element_type x9 -> x0, other arithmetic: 3.96 us -> none  [the longest x8 2.38 us: head_step(): probs_b = probs.astype(jnp.bfloat16)]
  transfers between devices with their start and end apart: 2 -> 0, of which waited for: 2 -> 0; matrix products, arithmetic and copies ran while one was open for 1% -> 0% of each run, Pallas kernels for 0% -> 0%
where the time goes in v2:
time: 68.8 us; the launch traced here: 68.6 us
  Pallas kernels  61.5 us (89%)
  local copies, waits for them, and re-layouts  6.36 us (9%)
    pallas_call x1, Pallas kernels, per_device(): pl.pallas_call(layer_kernel, name='layer', out_shape=(jax.ShapeDtypeStruc...  61.5 us
    unnamed x4, local copies, waits for them, and re-layouts  6.36 us

profile of v2, /device:TPU:1, one launch (start us, length us, event | category | flops | bytes accessed | tf_op | source)
XLA Modules:
  0.0 68.6 jit_solution(9148632317216038554)
XLA Ops:
  0.6 61.5 %layer.1 = (bf16[256,1024]{1,0:T(8,128)(2,1)}, bf16[256,128]{1,0:T(8,128)(2,1)}, bf16[256,128]{1,0:T(8,128)(2,1)}, bf16[50,1024]{1,0:T(8,128)(2,1)}) custom-call(bf16[256,1024]{1,0:T(8,128)(2,1)} %q_hbm.1, bf16[256,1024]{1,0:T(8,128)(2,1)} %g_hbm.1, bf16[256,128]{1,0:T(8,128)(2,1)} %ko_hbm.1, bf16[256,128]{1,0:T(8,128)(2,1)} %vo_hbm.1, ...), custom_call_target="tpu_custom_call" | custom-call | tf_op jit(solution)/shard_map/layer/pallas_call | solution.py:356
  62.2 1.9 %copy.16 = bf16[256,1024]{1,0:T(8,128)(2,1)} copy(bf16[256,1024]{1,0:T(8,128)(2,1)} %get-tuple-element.8) | data formatting | bytes 1048576
  64.1 1.5 %copy.17 = bf16[256,128]{1,0:T(8,128)(2,1)} copy(bf16[256,128]{1,0:T(8,128)(2,1)} %get-tuple-element.9) | data formatting | bytes 131072
  65.5 1.5 %copy.18 = bf16[256,128]{1,0:T(8,128)(2,1)} copy(bf16[256,128]{1,0:T(8,128)(2,1)} %get-tuple-element.10) | data formatting | bytes 131072
  67.0 1.6 %copy.19 = bf16[50,1024]{1,0:T(8,128)(2,1)} copy(bf16[50,1024]{1,0:T(8,128)(2,1)} %get-tuple-element.11) | data formatting | bytes 204800

commit v3 on v2

--- a/solution.py
+++ b/solution.py
@@ -16,6 +16,7 @@
 TILE = 16
 NX, NZ = 4, 8
 NTP = 8
+NY = NTP // 2
 GROUP = NZ * M
 REM0 = NZ * MAIN
 BLOCK = MAIN + TILE
@@ -77,14 +78,23 @@
     dq_hbm, dko_hbm, dvo_hbm, out_ref,
     q_ref, g_ref, ko_ref, vo_ref, st, w, sg_ref,
     mine, zrecv, grp, s_own, p_own, s_all, p_all, m_ref, l_ref, d_ref, dqt, kt_own, kt,
-    dk_acc, dv_acc, part, xback, acc, zsend, zback, em, tsend, trecv, dq_ref, dko_ref, dvo_ref,
-    wsem, insem, outsem, zs, zr, xs, xr, xbs, xbr, zbs, zbr, ts, tr,
+    dk_acc, dv_acc, part, xback, acc, zsend, zback, em, etwin, wtwin, state, tsend, trecv, dq_ref, dko_ref, dvo_ref,
+    wsem, insem, outsem, zs, zr, xs, xr, xbs, xbr, zbs, zbr, ts, tr, ws, wr, es, er,
 ):
     x, z = seg_place()
     tp = lax.axis_index("tp")
     peers = [{"seg": z_peer(x, z, d)[1]} for d in range(1, NZ)]
     peers += [{"seg": x_peer(x, z, d)[1]} for d in range(1, NX)]
-    peers += [{"tp": lax.rem(tp + d, NTP)} for d in range(1, NTP)]
+    core = lax.rem(tp, 2)
+    y = tp // 2
+    twin = tp + 1 - 2 * core
+
+    def y_peer(d):
+        other = lax.rem(y + d, NY)
+        return other, 2 * other + core
+
+    peers += [{"tp": twin}] + [{"tp": y_peer(d)[1]} for d in range(1, NY)]
+    last = x == NX - 1
     barrier, count = greet(peers)
 
     loads = []
@@ -133,7 +143,27 @@
         )
 
     for d in range(1, NZ):
-        zcopy(d, z_peer(x, z, d)[1], z).start()
+        other, peer = z_peer(x, z, d)
+
+        @pl.when(jnp.logical_not(last) | (other > z))
+        def _(d=d, peer=peer):
+            zcopy(d, peer, z).start()
+
+    cols = D // NTP
+
+    def wcopy(i):
+        rows_out = pl.ds(pl.multiple_of((2 * i + 1 - core) * cols, cols), cols)
+        return pltpu.make_async_remote_copy(
+            src_ref=w.at[rows_out],
+            dst_ref=wtwin.at[i],
+            send_sem=ws.at[i],
+            recv_sem=wr.at[i],
+            device_id={"tp": twin},
+            device_id_type=MESH,
+        )
+
+    for i in range(NY):
+        wcopy(i).start()
 
     def head(ref, h):
         return ref[:, h * HD : (h + 1) * HD]
@@ -143,7 +173,7 @@
 
     def sweep_one(keys, vals, s_ref, p_ref, mask, first):
         for h in range(HEADS):
-            s = dot(keys, head(q_ref, h), LAST)
+            s = dot(keys, head(q_ref, h), LAST) * SCALE2
             if mask is not None:
                 s = jnp.where(mask, s, NEG)
             s_ref[:, lanes(h)] = s
@@ -153,11 +183,11 @@
             if not first:
                 old = m_ref[:, lanes(h)]
                 top = jnp.maximum(old, top)
-            e = jnp.exp2(s * SCALE2 - top * SCALE2)
+            e = jnp.exp2(s - top)
             total = jnp.sum(e, axis=0, keepdims=True)
             inner = jnp.sum(e * p, axis=0, keepdims=True)
             if not first:
-                fade = jnp.exp2((old - top) * SCALE2)
+                fade = jnp.exp2(old - top)
                 total = total + l_ref[:, lanes(h)] * fade
                 inner = inner + d_ref[:, lanes(h)] * fade
             m_ref[:, lanes(h)] = top
@@ -169,7 +199,7 @@
         dk = dk_acc.at[0:count]
         dv = dv_acc.at[0:count]
         for h in range(HEADS):
-            probs = jnp.exp2(s_ref[:, lanes(h)] * SCALE2 - m_ref[:, lanes(h)])
+            probs = jnp.exp2(s_ref[:, lanes(h)] - m_ref[:, lanes(h)])
             ds = (probs * (p_ref[:, lanes(h)] - d_ref[:, lanes(h)])).astype(BF16)
             dv_new = dot(probs.astype(BF16), head(g_ref, h))
             dk_new = dot(ds, head(q_ref, h))
@@ -191,14 +221,25 @@
     dqt[...] = jnp.zeros_like(dqt)
     sweep_one(ko_ref[...], vo_ref[...], s_own, p_own, tri, True)
 
-    grp[x, pl.ds(pl.multiple_of(z * MAIN, TILE), MAIN), :] = mine[0:MAIN, :]
-    shared = mine[MAIN:BLOCK, :].astype(F32)
-    for d in range(1, NZ):
-        other, peer = z_peer(x, z, NZ - d)
-        zcopy(d, peer, other).wait_recv()
-        grp[x, pl.ds(pl.multiple_of(other * MAIN, TILE), MAIN), :] = zrecv[other, 0:MAIN, :]
-        shared = shared + zrecv[other, MAIN:BLOCK, :].astype(F32)
-    grp[x, REM0:GROUP, :] = shared.astype(BF16)
+    def assemble():
+        grp[x, pl.ds(pl.multiple_of(z * MAIN, TILE), MAIN), :] = mine[0:MAIN, :]
+        acc[0:TILE, :] = mine[MAIN:BLOCK, :].astype(F32)
+        for d in range(1, NZ):
+            other, peer = z_peer(x, z, NZ - d)
+            sent = jnp.logical_not(last) | (other < z)
+            place = pl.ds(pl.multiple_of(other * MAIN, TILE), MAIN)
+
+            @pl.when(sent)
+            def _(d=d, other=other, peer=peer, place=place):
+                zcopy(d, peer, other).wait_recv()
+                grp[x, place, :] = zrecv[other, 0:MAIN, :]
+                acc[0:TILE, :] += zrecv[other, MAIN:BLOCK, :].astype(F32)
+
+            @pl.when(jnp.logical_not(sent))
+            def _(place=place):
+                grp[x, place, :] = jnp.zeros((MAIN, W2), BF16)
+
+        grp[x, REM0:GROUP, :] = acc[0:TILE, :].astype(BF16)
 
     def xcopy(d, g):
         other = lax.rem(x + d + NX, NX)
@@ -211,7 +252,22 @@
             device_id_type=MESH,
         )
 
-    lax.fori_loop(1, NX - x, lambda d, c: (xcopy(d, x).start(), c)[1], 0)
+    @pl.when(jnp.logical_not(last))
+    def _():
+        assemble()
+        lax.fori_loop(1, NX - x, lambda d, c: (xcopy(d, x).start(), c)[1], 0)
+
+    def full_group(d, carry):
+        g = x - d
+        xcopy(-d, g).wait_recv()
+        sweep_one(grp[g, :, 0:HD], grp[g, :, HD:W2], s_all.at[g], p_all.at[g], None, False)
+        return carry
+
+    lax.fori_loop(1, x + 1, full_group, 0)
+
+    @pl.when(last)
+    def _():
+        assemble()
 
     @pl.when(z > 0)
     def _():
@@ -219,15 +275,8 @@
         mask = (r < MAIN * z) | ((r >= REM0) & (r < REM0 + REM * z))
         sweep_one(grp[x, :, 0:HD], grp[x, :, HD:W2], s_all.at[x], p_all.at[x], mask, False)
 
-    def full_group(d, carry):
-        g = x - d
-        xcopy(-d, g).wait_recv()
-        sweep_one(grp[g, :, 0:HD], grp[g, :, HD:W2], s_all.at[g], p_all.at[g], None, False)
-        return carry
-
-    lax.fori_loop(1, x + 1, full_group, 0)
     d_ref[...] = d_ref[...] / l_ref[...]
-    m_ref[...] = m_ref[...] * SCALE2 + jnp.log2(l_ref[...])
+    m_ref[...] = m_ref[...] + jnp.log2(l_ref[...])
 
     def xback_copy(d, g):
         other = lax.rem(x + d + NX, NX)
@@ -243,7 +292,8 @@
 
     acc[...] = jnp.zeros_like(acc)
 
-    def back_group(g, carry):
+    def back_group(i, carry):
+        g = jnp.where(i < x, lax.rem(i + 1, jnp.maximum(x, 1)), x)
         kt[...] = grp[g, :, 0:HD].astype(F32).T.astype(BF16)
         dk, dv = sweep_two(s_all.at[g], p_all.at[g], kt)
 
@@ -284,7 +334,11 @@
         )
 
     for d in range(1, NZ):
-        zback_copy(d, *z_peer(x, z, d)).start()
+        other, peer = z_peer(x, z, d)
+
+        @pl.when(jnp.logical_not(last) | (other < z))
+        def _(d=d, other=other, peer=peer):
+            zback_copy(d, other, peer).start()
 
     dk, dv = sweep_two(s_own, p_own, kt_own)
     dko_ref[...] = dk.astype(BF16)
@@ -298,21 +352,42 @@
     for copy in stores:
         copy.start()
 
-    total = zsend[z].astype(F32)
+    mine_acc = acc.at[0:BLOCK]
+    mine_acc[...] = zsend[z].astype(F32)
     for d in range(1, NZ):
-        zback_copy(d, *z_peer(x, z, NZ - d)).wait_recv()
-        total = total + zback[d - 1].astype(F32)
+        other, peer = z_peer(x, z, NZ - d)
+
+        @pl.when(jnp.logical_not(last) | (other > z))
+        def _(d=d, other=other, peer=peer):
+            zback_copy(d, other, peer).wait_recv()
+            mine_acc[...] += zback[d - 1].astype(F32)
+
+    total = mine_acc[...]
     rem = total[MAIN:BLOCK]
     one = jnp.sum(jnp.where(row == REM * z, rem, 0.0), axis=0, keepdims=True)
     two = jnp.sum(jnp.where(row == REM * z + 1, rem, 0.0), axis=0, keepdims=True)
     em[0:MAIN, :] = total[0:MAIN].astype(BF16)
     em[MAIN:BLOCK, :] = jnp.where(row == 0, one, jnp.where(row == 1, two, 0.0)).astype(BF16)
 
-    cols = D // NTP
-
-    def state(target):
+    def ecopy():
+        return pltpu.make_async_remote_copy(
+            src_ref=em,
+            dst_ref=etwin,
+            send_sem=es,
+            recv_sem=er,
+            device_id={"tp": twin},
+            device_id_type=MESH,
+        )
+
+    ecopy().start()
+    order = (2, 1, 3, 0)
+    for d in order:
+        target = y_peer(d)[1]
         chunk = pl.ds(pl.multiple_of(target * cols, cols), cols)
-        return dot(em[...], w[chunk, :], LAST)[0:M]
+        state[d] = dot(em[...], w[chunk, :], LAST)
+    for i in range(NY):
+        wcopy(i).wait_recv()
+    ecopy().wait_recv()
 
     def tcopy(d, target):
         return pltpu.make_async_remote_copy(
@@ -324,13 +399,15 @@
             device_id_type=MESH,
         )
 
-    for d in range(1, NTP):
-        target = lax.rem(tp + d, NTP)
-        tsend[d - 1] = state(target).astype(BF16)
-        tcopy(d, target).start()
-    out = state(tp) + sg_ref[...].astype(F32)
-    for d in range(1, NTP):
-        tcopy(d, lax.rem(tp + NTP - d, NTP)).wait_recv()
+    for d in order:
+        other, target = y_peer(d)
+        both = (state[d] + dot(etwin[...], wtwin[other], LAST))[0:M]
+        if d:
+            tsend[d - 1] = both.astype(BF16)
+            tcopy(d, target).start()
+    out = both + sg_ref[...].astype(F32)
+    for d in (1, 3, 2):
+        tcopy(d, y_peer(NY - d)[1]).wait_recv()
         out = out + trecv[d - 1].astype(F32)
     out_ref[...] = out.astype(BF16)
 
@@ -338,12 +415,45 @@
         copy.wait()
     for d in range(1, NZ):
         other, peer = z_peer(x, z, d)
-        zcopy(d, peer, z).wait_send()
-        zback_copy(d, other, peer).wait_send()
+
+        @pl.when(jnp.logical_not(last) | (other > z))
+        def _(d=d, peer=peer):
+            zcopy(d, peer, z).wait_send()
+
+        @pl.when(jnp.logical_not(last) | (other < z))
+        def _(d=d, other=other, peer=peer):
+            zback_copy(d, other, peer).wait_send()
+
     lax.fori_loop(1, NX - x, lambda d, c: (xcopy(d, x).wait_send(), c)[1], 0)
     lax.fori_loop(1, x + 1, lambda d, c: (xback_copy(-d, x - d).wait_send(), c)[1], 0)
-    for d in range(1, NTP):
-        tcopy(d, lax.rem(tp + d, NTP)).wait_send()
+    for i in range(NY):
+        wcopy(i).wait_send()
+    ecopy().wait_send()
+    for d in range(1, NY):
+        tcopy(d, y_peer(d)[1]).wait_send()
+
+
+def emit_kernel(*refs):
+    count = (len(refs) - 1) // 2
+    copies = [
+        pltpu.make_async_copy(refs[i], refs[count + i], refs[-1].at[i]) for i in range(count)
+    ]
+    for copy in copies:
+        copy.start()
+    for copy in copies:
+        copy.wait()
+
+
+def emit(arrays):
+    anywhere = pl.BlockSpec(memory_space=pl.ANY)
+    return pl.pallas_call(
+        emit_kernel,
+        name="emit",
+        out_shape=tuple(jax.ShapeDtypeStruct(a.shape, a.dtype) for a in arrays),
+        in_specs=[anywhere] * len(arrays),
+        out_specs=(anywhere,) * len(arrays),
+        scratch_shapes=[pltpu.SemaphoreType.DMA((len(arrays),))],
+    )(*arrays)
 
 
 def per_device(
@@ -353,7 +463,7 @@
     rows = HEADS * TOK
     cols = D // NTP
     dma = pltpu.SemaphoreType.DMA
-    return pl.pallas_call(
+    arrays = pl.pallas_call(
         layer_kernel,
         name="layer",
         out_shape=(
@@ -393,8 +503,11 @@
             pltpu.VMEM((NZ, BLOCK, W2), BF16),
             pltpu.VMEM((NZ - 1, BLOCK, W2), BF16),
             pltpu.VMEM((BLOCK, W2), BF16),
-            pltpu.VMEM((NTP - 1, M, cols), BF16),
-            pltpu.VMEM((NTP - 1, M, cols), BF16),
+            pltpu.VMEM((BLOCK, W2), BF16),
+            pltpu.VMEM((NY, cols, W2), BF16),
+            pltpu.VMEM((NY, BLOCK, cols), F32),
+            pltpu.VMEM((NY - 1, M, cols), BF16),
+            pltpu.VMEM((NY - 1, M, cols), BF16),
             pltpu.VMEM((TOK, HEADS * HD), BF16),
             pltpu.VMEM((TOK, HD), BF16),
             pltpu.VMEM((TOK, HD), BF16),
@@ -409,8 +522,12 @@
             dma((NX - 1,)),
             dma((NZ - 1,)),
             dma((NZ - 1,)),
-            dma((NTP - 1,)),
-            dma((NTP - 1,)),
+            dma((NY - 1,)),
+            dma((NY - 1,)),
+            dma((NY,)),
+            dma((NY,)),
+            dma,
+            dma,
         ],
         compiler_params=pltpu.CompilerParams(
             collective_id=0, has_side_effects=True, vmem_limit_bytes=58 << 20
@@ -418,6 +535,7 @@
     )(
         queries, out_grad, keys_own, values_own, summary_states, w_key, w_value, summary_grad
     )
+    return emit(arrays)
 
 
 def solution(mesh):

time: 68.8 us -> 87.3 us (1.27)
  Pallas kernels: 61.5 us -> 86.5 us
  local copies, waits for them, and re-layouts: 6.36 us -> 0 us
    pallas_call x0 -> x1, Pallas kernels: none -> 24.5 us  [emit(): pl.pallas_call(emit_kernel, name='emit', out_shape=tuple((jax.ShapeDtypeS...]
    unnamed x4 -> x0, local copies, waits for them, and re-layouts: 6.36 us -> none
where the time goes in v3:
time: 87.3 us; the launch traced here: 87.2 us
  Pallas kernels  86.5 us (99%)
    pallas_call x1, Pallas kernels, per_device(): pl.pallas_call(layer_kernel, name='layer', out_shape=(jax.ShapeDtypeStruc...  62.1 us
    pallas_call x1, Pallas kernels, emit(): pl.pallas_call(emit_kernel, name='emit', out_shape=tuple((jax.ShapeDtypeS...  24.5 us

profile of v3, /device:TPU:1, one launch (start us, length us, event | category | flops | bytes accessed | tf_op | source)
XLA Modules:
  0.0 87.2 jit_solution(10273014823799614948)
XLA Ops:
  0.6 62.1 %layer.1 = (bf16[256,1024]{1,0:T(8,128)(2,1)}, bf16[256,128]{1,0:T(8,128)(2,1)}, bf16[256,128]{1,0:T(8,128)(2,1)}, bf16[50,1024]{1,0:T(8,128)(2,1)}) custom-call(bf16[256,1024]{1,0:T(8,128)(2,1)} %q_hbm.1, bf16[256,1024]{1,0:T(8,128)(2,1)} %g_hbm.1, bf16[256,128]{1,0:T(8,128)(2,1)} %ko_hbm.1, bf16[256,128]{1,0:T(8,128)(2,1)} %vo_hbm.1, ...), custom_call_target="tpu_custom_call" | custom-call | tf_op jit(solution)/shard_map/layer/pallas_call | solution.py:466
  62.7 24.5 %emit.1 = (bf16[256,1024]{1,0:T(8,128)(2,1)}, bf16[256,128]{1,0:T(8,128)(2,1)}, bf16[256,128]{1,0:T(8,128)(2,1)}, bf16[50,1024]{1,0:T(8,128)(2,1)}) custom-call(bf16[256,1024]{1,0:T(8,128)(2,1)} %get-tuple-element.8.refs_0_, bf16[256,128]{1,0:T(8,128)(2,1)} %get-tuple-element.9.refs_1_, bf16[256,128]{1,0:T(8,128)(2,1)} %get-tuple-element.10.refs_2_, ...), custom_call_target="tpu_custom_call" | custom-call | tf_op jit(solution)/shard_map/emit/pallas_call | solution.py:449

commit v4 on v3

--- a/solution.py
+++ b/solution.py
@@ -1,3 +1,4 @@
+import functools
 import math
 
 import jax
@@ -132,22 +133,94 @@
     mine[MAIN:BLOCK, :] = shared.astype(BF16)
     pl.semaphore_wait(barrier, count)
 
-    def zcopy(d, peer, slot):
-        return pltpu.make_async_remote_copy(
-            src_ref=mine,
-            dst_ref=zrecv.at[slot],
-            send_sem=zs.at[d - 1],
-            recv_sem=zr.at[d - 1],
-            device_id={"seg": peer},
-            device_id_type=MESH,
-        )
-
-    for d in range(1, NZ):
+    def rows_of(i):
+        return pl.ds(pl.multiple_of(i * MAIN, TILE), MAIN)
+
+    def zcopies(d, peer, slot):
+        own = {"device_id": {"seg": peer}, "device_id_type": MESH}
+        return (
+            pltpu.make_async_remote_copy(
+                src_ref=mine.at[0:MAIN],
+                dst_ref=grp.at[x, rows_of(slot)],
+                send_sem=zs.at[0, d - 1],
+                recv_sem=zr.at[0, d - 1],
+                **own,
+            ),
+            pltpu.make_async_remote_copy(
+                src_ref=mine.at[MAIN:BLOCK],
+                dst_ref=zrecv.at[slot],
+                send_sem=zs.at[1, d - 1],
+                recv_sem=zr.at[1, d - 1],
+                **own,
+            ),
+        )
+
+    near = (1, 7, 2, 6, 3, 5, 4)
+    for d in near:
         other, peer = z_peer(x, z, d)
 
         @pl.when(jnp.logical_not(last) | (other > z))
         def _(d=d, peer=peer):
-            zcopy(d, peer, z).start()
+            for copy in zcopies(d, peer, z):
+                copy.start()
+
+    def xcopy(d, g, part_rows=None):
+        other = lax.rem(x + d + NX, NX)
+        ref = grp.at[g] if part_rows is None else grp.at[g, part_rows]
+        return pltpu.make_async_remote_copy(
+            src_ref=ref,
+            dst_ref=ref,
+            send_sem=xs.at[jnp.abs(d) - 1],
+            recv_sem=xr.at[jnp.abs(d) - 1],
+            device_id={"seg": other * NZ + z},
+            device_id_type=MESH,
+        )
+
+    def pass_on(part_rows):
+        for d in (3, 1, 2):
+            @pl.when((x + d < NX) & ((x > 0) | (d != 2)))
+            def _(d=d):
+                xcopy(d, x, part_rows).start()
+
+    grp[x, rows_of(z), :] = mine[0:MAIN, :]
+    pass_on(rows_of(z))
+
+    def assemble(sent_on):
+        acc[0:TILE, :] = mine[MAIN:BLOCK, :].astype(F32)
+        for d in near:
+            other, peer = z_peer(x, z, NZ - d)
+            if sent_on:
+                zcopies(d, peer, other)[0].wait_recv()
+                pass_on(rows_of(other))
+            else:
+
+                @pl.when(other < z)
+                def _(d=d, other=other, peer=peer):
+                    zcopies(d, peer, other)[0].wait_recv()
+
+                @pl.when(other > z)
+                def _(other=other):
+                    grp[x, rows_of(other), :] = jnp.zeros((MAIN, W2), BF16)
+
+        for d in near:
+            other, peer = z_peer(x, z, NZ - d)
+
+            @pl.when(jnp.bool_(sent_on) | (other < z))
+            def _(d=d, other=other, peer=peer):
+                zcopies(d, peer, other)[1].wait_recv()
+                acc[0:TILE, :] += zrecv[other].astype(F32)
+
+        grp[x, REM0:GROUP, :] = acc[0:TILE, :].astype(BF16)
+        if sent_on:
+            pass_on(pl.ds(REM0, TILE))
+
+            @pl.when(x == 0)
+            def _():
+                xcopy(2, x).start()
+
+    @pl.when(jnp.logical_not(last))
+    def _():
+        assemble(True)
 
     cols = D // NTP
 
@@ -221,43 +294,8 @@
     dqt[...] = jnp.zeros_like(dqt)
     sweep_one(ko_ref[...], vo_ref[...], s_own, p_own, tri, True)
 
-    def assemble():
-        grp[x, pl.ds(pl.multiple_of(z * MAIN, TILE), MAIN), :] = mine[0:MAIN, :]
-        acc[0:TILE, :] = mine[MAIN:BLOCK, :].astype(F32)
-        for d in range(1, NZ):
-            other, peer = z_peer(x, z, NZ - d)
-            sent = jnp.logical_not(last) | (other < z)
-            place = pl.ds(pl.multiple_of(other * MAIN, TILE), MAIN)
-
-            @pl.when(sent)
-            def _(d=d, other=other, peer=peer, place=place):
-                zcopy(d, peer, other).wait_recv()
-                grp[x, place, :] = zrecv[other, 0:MAIN, :]
-                acc[0:TILE, :] += zrecv[other, MAIN:BLOCK, :].astype(F32)
-
-            @pl.when(jnp.logical_not(sent))
-            def _(place=place):
-                grp[x, place, :] = jnp.zeros((MAIN, W2), BF16)
-
-        grp[x, REM0:GROUP, :] = acc[0:TILE, :].astype(BF16)
-
-    def xcopy(d, g):
-        other = lax.rem(x + d + NX, NX)
-        return pltpu.make_async_remote_copy(
-            src_ref=grp.at[g],
-            dst_ref=grp.at[g],
-            send_sem=xs.at[jnp.abs(d) - 1],
-            recv_sem=xr.at[jnp.abs(d) - 1],
-            device_id={"seg": other * NZ + z},
-            device_id_type=MESH,
-        )
-
-    @pl.when(jnp.logical_not(last))
-    def _():
-        assemble()
-        lax.fori_loop(1, NX - x, lambda d, c: (xcopy(d, x).start(), c)[1], 0)
-
-    def full_group(d, carry):
+    def full_group(i, carry):
+        d = jnp.where(last & (i > 1), 5 - i, i)
         g = x - d
         xcopy(-d, g).wait_recv()
         sweep_one(grp[g, :, 0:HD], grp[g, :, HD:W2], s_all.at[g], p_all.at[g], None, False)
@@ -267,7 +305,7 @@
 
     @pl.when(last)
     def _():
-        assemble()
+        assemble(False)
 
     @pl.when(z > 0)
     def _():
@@ -278,46 +316,55 @@
     d_ref[...] = d_ref[...] / l_ref[...]
     m_ref[...] = m_ref[...] + jnp.log2(l_ref[...])
 
-    def xback_copy(d, g):
-        other = lax.rem(x + d + NX, NX)
-        slot = jnp.abs(d) - 1
+    def hop(g, peer_x, wrap):
         return pltpu.make_async_remote_copy(
             src_ref=part.at[g],
-            dst_ref=xback.at[slot],
-            send_sem=xbs.at[slot],
-            recv_sem=xbr.at[slot],
-            device_id={"seg": other * NZ + z},
+            dst_ref=xback.at[jnp.where(wrap, NX - 1, g)],
+            send_sem=xbs.at[g],
+            recv_sem=xbr.at[jnp.where(wrap, NX - 1, g)],
+            device_id={"seg": peer_x * NZ + z},
             device_id_type=MESH,
         )
 
-    acc[...] = jnp.zeros_like(acc)
+    def hop_out(g):
+        wrap = last & (g == 0)
+        return hop(g, jnp.where(wrap, 0, x - 1), wrap)
+
+    def hop_add(g, peer_x, wrap):
+        hop(g, peer_x, wrap).wait_recv()
+        acc[...] += xback[jnp.where(wrap, NX - 1, g)].astype(F32)
 
     def back_group(i, carry):
-        g = jnp.where(i < x, lax.rem(i + 1, jnp.maximum(x, 1)), x)
+        g = jnp.where(last & (i < 2), 1 - i, i)
         kt[...] = grp[g, :, 0:HD].astype(F32).T.astype(BF16)
         dk, dv = sweep_two(s_all.at[g], p_all.at[g], kt)
+        acc[:, 0:HD] = dk
+        acc[:, HD:W2] = dv
 
         @pl.when(g < x)
         def _():
-            part[g, :, 0:HD] = dk.astype(BF16)
-            part[g, :, HD:W2] = dv.astype(BF16)
-            xback_copy(g - x, g).start()
-
-        @pl.when(g == x)
-        def _():
-            acc[:, 0:HD] = dk
-            acc[:, HD:W2] = dv
+            @pl.when((x == 1) | ((x == 2) & (g == 1)))
+            def _():
+                hop_add(g, x + 1, False)
+
+            part[g] = acc[...].astype(BF16)
+            hop_out(g).start()
 
         return carry
 
     lax.fori_loop(0, x + jnp.minimum(z, 1), back_group, 0)
 
-    def add_group(d, carry):
-        xback_copy(d, x).wait_recv()
-        acc[...] += xback[d - 1].astype(F32)
-        return carry
-
-    lax.fori_loop(1, NX - x, add_group, 0)
+    @pl.when(z == 0)
+    def _():
+        acc[...] = jnp.zeros_like(acc)
+
+    @pl.when(jnp.logical_not(last))
+    def _():
+        hop_add(x, x + 1, False)
+
+    @pl.when(x == 0)
+    def _():
+        hop_add(x, NX - 1, True)
 
     for i in range(NZ):
         zsend[i, 0:MAIN, :] = acc[i * MAIN : (i + 1) * MAIN, :].astype(BF16)
@@ -418,14 +465,15 @@
 
         @pl.when(jnp.logical_not(last) | (other > z))
         def _(d=d, peer=peer):
-            zcopy(d, peer, z).wait_send()
+            for copy in zcopies(d, peer, z):
+                copy.wait_send()
 
         @pl.when(jnp.logical_not(last) | (other < z))
         def _(d=d, other=other, peer=peer):
             zback_copy(d, other, peer).wait_send()
 
     lax.fori_loop(1, NX - x, lambda d, c: (xcopy(d, x).wait_send(), c)[1], 0)
-    lax.fori_loop(1, x + 1, lambda d, c: (xback_copy(-d, x - d).wait_send(), c)[1], 0)
+    lax.fori_loop(0, x, lambda g, c: (hop_out(g).wait_send(), c)[1], 0)
     for i in range(NY):
         wcopy(i).wait_send()
     ecopy().wait_send()
@@ -433,26 +481,31 @@
         tcopy(d, y_peer(d)[1]).wait_send()
 
 
-def emit_kernel(*refs):
-    count = (len(refs) - 1) // 2
-    copies = [
-        pltpu.make_async_copy(refs[i], refs[count + i], refs[-1].at[i]) for i in range(count)
-    ]
-    for copy in copies:
+def emit_kernel(count, *refs):
+    ins, outs, bufs = refs[:count], refs[count : 2 * count], refs[2 * count : 3 * count]
+    sems = refs[3 * count]
+    loads = [pltpu.make_async_copy(ins[i], bufs[i], sems.at[0, i]) for i in range(count)]
+    stores = [pltpu.make_async_copy(bufs[i], outs[i], sems.at[1, i]) for i in range(count)]
+    for copy in loads:
         copy.start()
-    for copy in copies:
+    for load, store in zip(loads, stores):
+        load.wait()
+        store.start()
+    for copy in stores:
         copy.wait()
 
 
 def emit(arrays):
     anywhere = pl.BlockSpec(memory_space=pl.ANY)
+    count = len(arrays)
     return pl.pallas_call(
-        emit_kernel,
+        functools.partial(emit_kernel, count),
         name="emit",
         out_shape=tuple(jax.ShapeDtypeStruct(a.shape, a.dtype) for a in arrays),
-        in_specs=[anywhere] * len(arrays),
-        out_specs=(anywhere,) * len(arrays),
-        scratch_shapes=[pltpu.SemaphoreType.DMA((len(arrays),))],
+        in_specs=[anywhere] * count,
+        out_specs=(anywhere,) * count,
+        scratch_shapes=[pltpu.VMEM(a.shape, a.dtype) for a in arrays]
+        + [pltpu.SemaphoreType.DMA((2, count))],
     )(*arrays)
 
 
@@ -483,7 +536,7 @@
             pltpu.VMEM((D, W2), BF16),
             pltpu.VMEM((M, cols), BF16),
             pltpu.VMEM((BLOCK, W2), BF16),
-            pltpu.VMEM((NZ, BLOCK, W2), BF16),
+            pltpu.VMEM((NZ, TILE, W2), BF16),
             pltpu.VMEM((NX, GROUP, W2), BF16),
             pltpu.VMEM((TOK, rows), F32),
             pltpu.VMEM((TOK, rows), F32),
@@ -498,7 +551,7 @@
             pltpu.VMEM((GROUP, HD), F32),
             pltpu.VMEM((GROUP, HD), F32),
             pltpu.VMEM((NX, GROUP, W2), BF16),
-            pltpu.VMEM((NX - 1, GROUP, W2), BF16),
+            pltpu.VMEM((NX, GROUP, W2), BF16),
             pltpu.VMEM((GROUP, W2), F32),
             pltpu.VMEM((NZ, BLOCK, W2), BF16),
             pltpu.VMEM((NZ - 1, BLOCK, W2), BF16),
@@ -514,12 +567,12 @@
             dma((WCHUNK, 2)),
             dma((6,)),
             dma((3,)),
-            dma((NZ - 1,)),
-            dma((NZ - 1,)),
+            dma((2, NZ - 1)),
+            dma((2, NZ - 1)),
             dma((NX - 1,)),
             dma((NX - 1,)),
             dma((NX - 1,)),
-            dma((NX - 1,)),
+            dma((NX,)),
             dma((NZ - 1,)),
             dma((NZ - 1,)),
             dma((NY - 1,)),

time: 87.3 us -> 59.4 us (0.68)
  Pallas kernels: 86.5 us -> 58.3 us
    pallas_call x1, Pallas kernels: 24.5 us -> 1.97 us  [emit(): pl.pallas_call(functools.partial(emit_kernel, count), name='emit', out_sh...]
    pallas_call x1, Pallas kernels: 62.1 us -> 56.3 us  [per_device(): pl.pallas_call(layer_kernel, name='layer', out_shape=(jax.ShapeDtypeStruc...]
where the time goes in v4:
time: 59.4 us; the launch traced here: 58.9 us
  Pallas kernels  58.3 us (98%)
  between operations  0.64 us (1%)
    pallas_call x1, Pallas kernels, per_device(): pl.pallas_call(layer_kernel, name='layer', out_shape=(jax.ShapeDtypeStruc...  56.3 us
    pallas_call x1, Pallas kernels, emit(): pl.pallas_call(functools.partial(emit_kernel, count), name='emit', out_sh...  1.97 us

profile of v4, /device:TPU:1, one launch (start us, length us, event | category | flops | bytes accessed | tf_op | source)
XLA Modules:
  0.0 58.9 jit_solution(5573476069495254124)
XLA Ops:
  0.6 56.3 %layer.1 = (bf16[256,1024]{1,0:T(8,128)(2,1)}, bf16[256,128]{1,0:T(8,128)(2,1)}, bf16[256,128]{1,0:T(8,128)(2,1)}, bf16[50,1024]{1,0:T(8,128)(2,1)}) custom-call(bf16[256,1024]{1,0:T(8,128)(2,1)} %q_hbm.1, bf16[256,1024]{1,0:T(8,128)(2,1)} %g_hbm.1, bf16[256,128]{1,0:T(8,128)(2,1)} %ko_hbm.1, bf16[256,128]{1,0:T(8,128)(2,1)} %vo_hbm.1, ...), custom_call_target="tpu_custom_call" | custom-call | tf_op jit(solution)/shard_map/layer/pallas_call | solution.py:519
  57.0 2.0 %emit.1 = (bf16[256,1024]{1,0:T(8,128)(2,1)}, bf16[256,128]{1,0:T(8,128)(2,1)}, bf16[256,128]{1,0:T(8,128)(2,1)}, bf16[50,1024]{1,0:T(8,128)(2,1)}) custom-call(bf16[256,1024]{1,0:T(8,128)(2,1)} %get-tuple-element.8.refs_0_, bf16[256,128]{1,0:T(8,128)(2,1)} %get-tuple-element.9.refs_1_, bf16[256,128]{1,0:T(8,128)(2,1)} %get-tuple-element.10.refs_2_, ...), custom_call_target="tpu_custom_call" | custom-call | tf_op jit(solution)/shard_map/emit/pallas_call | solution.py:501

commit v5 on v4

--- a/solution.py
+++ b/solution.py
@@ -21,6 +21,7 @@
 GROUP = NZ * M
 REM0 = NZ * MAIN
 BLOCK = MAIN + TILE
+HALF = REM0 // 2
 D = 8192
 W2 = 2 * HD
 SCALE = HD ** (-0.5)
@@ -79,7 +80,7 @@
     dq_hbm, dko_hbm, dvo_hbm, out_ref,
     q_ref, g_ref, ko_ref, vo_ref, st, w, sg_ref,
     mine, zrecv, grp, s_own, p_own, s_all, p_all, m_ref, l_ref, d_ref, dqt, kt_own, kt,
-    dk_acc, dv_acc, part, xback, acc, zsend, zback, em, etwin, wtwin, state, tsend, trecv, dq_ref, dko_ref, dvo_ref,
+    dk_acc, dv_acc, part, xback, acc, zmain, zrem, zback, zback_rem, em, etwin, wtwin, state, tsend, trecv, dq_ref, dko_ref, dvo_ref,
     wsem, insem, outsem, zs, zr, xs, xr, xbs, xbr, zbs, zbr, ts, tr, ws, wr, es, er,
 ):
     x, z = seg_place()
@@ -316,23 +317,27 @@
     d_ref[...] = d_ref[...] / l_ref[...]
     m_ref[...] = m_ref[...] + jnp.log2(l_ref[...])
 
-    def hop(g, peer_x, wrap):
+    pieces = (pl.ds(0, HALF), pl.ds(HALF, GROUP - HALF))
+
+    def hop(g, piece, peer_x, wrap):
+        slot = jnp.where(wrap, NX - 1, g)
         return pltpu.make_async_remote_copy(
-            src_ref=part.at[g],
-            dst_ref=xback.at[jnp.where(wrap, NX - 1, g)],
-            send_sem=xbs.at[g],
-            recv_sem=xbr.at[jnp.where(wrap, NX - 1, g)],
+            src_ref=part.at[g, pieces[piece]],
+            dst_ref=xback.at[slot, pieces[piece]],
+            send_sem=xbs.at[g, piece],
+            recv_sem=xbr.at[slot, piece],
             device_id={"seg": peer_x * NZ + z},
             device_id_type=MESH,
         )
 
-    def hop_out(g):
+    def hop_out(g, piece):
         wrap = last & (g == 0)
-        return hop(g, jnp.where(wrap, 0, x - 1), wrap)
-
-    def hop_add(g, peer_x, wrap):
-        hop(g, peer_x, wrap).wait_recv()
-        acc[...] += xback[jnp.where(wrap, NX - 1, g)].astype(F32)
+        return hop(g, piece, jnp.where(wrap, 0, x - 1), wrap)
+
+    def hop_add(g, piece, peer_x, wrap):
+        hop(g, piece, peer_x, wrap).wait_recv()
+        rows_in = pieces[piece]
+        acc[rows_in, :] += xback[jnp.where(wrap, NX - 1, g), rows_in, :].astype(F32)
 
     def back_group(i, carry):
         g = jnp.where(last & (i < 2), 1 - i, i)
@@ -343,12 +348,14 @@
 
         @pl.when(g < x)
         def _():
-            @pl.when((x == 1) | ((x == 2) & (g == 1)))
-            def _():
-                hop_add(g, x + 1, False)
-
-            part[g] = acc[...].astype(BF16)
-            hop_out(g).start()
+            for piece in range(2):
+
+                @pl.when((x == 1) | ((x == 2) & (g == 1)))
+                def _(piece=piece):
+                    hop_add(g, piece, x + 1, False)
+
+                part[g, pieces[piece], :] = acc[pieces[piece], :].astype(BF16)
+                hop_out(g, piece).start()
 
         return carry
 
@@ -358,34 +365,52 @@
     def _():
         acc[...] = jnp.zeros_like(acc)
 
-    @pl.when(jnp.logical_not(last))
-    def _():
-        hop_add(x, x + 1, False)
-
-    @pl.when(x == 0)
-    def _():
-        hop_add(x, NX - 1, True)
-
+    def zmain_copy(source, target):
+        return pltpu.make_async_remote_copy(
+            src_ref=zmain.at[target],
+            dst_ref=zback.at[source],
+            send_sem=zbs.at[0, target],
+            recv_sem=zbr.at[0, source],
+            device_id={"seg": x * NZ + target},
+            device_id_type=MESH,
+        )
+
+    def zrem_copy(source, target):
+        return pltpu.make_async_remote_copy(
+            src_ref=zrem,
+            dst_ref=zback_rem.at[source],
+            send_sem=zbs.at[1, target],
+            recv_sem=zbr.at[1, source],
+            device_id={"seg": x * NZ + target},
+            device_id_type=MESH,
+        )
+
+    def sends(source, target):
+        return (source != target) & (jnp.logical_not(last) | (target < source))
+
+    for piece in range(2):
+
+        @pl.when(jnp.logical_not(last))
+        def _(piece=piece):
+            hop_add(x, piece, x + 1, False)
+
+        @pl.when(x == 0)
+        def _(piece=piece):
+            hop_add(x, piece, NX - 1, True)
+
+        for i in range(piece * NZ // 2, (piece + 1) * NZ // 2):
+            zmain[i] = acc[i * MAIN : (i + 1) * MAIN, :].astype(BF16)
+
+            @pl.when(sends(z, i))
+            def _(i=i):
+                zmain_copy(z, i).start()
+
+    zrem[...] = acc[REM0:GROUP, :].astype(BF16)
     for i in range(NZ):
-        zsend[i, 0:MAIN, :] = acc[i * MAIN : (i + 1) * MAIN, :].astype(BF16)
-        zsend[i, MAIN:BLOCK, :] = acc[REM0:GROUP, :].astype(BF16)
-
-    def zback_copy(d, other, peer):
-        return pltpu.make_async_remote_copy(
-            src_ref=zsend.at[other],
-            dst_ref=zback.at[d - 1],
-            send_sem=zbs.at[d - 1],
-            recv_sem=zbr.at[d - 1],
-            device_id={"seg": peer},
-            device_id_type=MESH,
-        )
-
-    for d in range(1, NZ):
-        other, peer = z_peer(x, z, d)
-
-        @pl.when(jnp.logical_not(last) | (other < z))
-        def _(d=d, other=other, peer=peer):
-            zback_copy(d, other, peer).start()
+
+        @pl.when(sends(z, i))
+        def _(i=i):
+            zrem_copy(z, i).start()
 
     dk, dv = sweep_two(s_own, p_own, kt_own)
     dko_ref[...] = dk.astype(BF16)
@@ -399,17 +424,23 @@
     for copy in stores:
         copy.start()
 
-    mine_acc = acc.at[0:BLOCK]
-    mine_acc[...] = zsend[z].astype(F32)
-    for d in range(1, NZ):
-        other, peer = z_peer(x, z, NZ - d)
-
-        @pl.when(jnp.logical_not(last) | (other > z))
-        def _(d=d, other=other, peer=peer):
-            zback_copy(d, other, peer).wait_recv()
-            mine_acc[...] += zback[d - 1].astype(F32)
-
-    total = mine_acc[...]
+    acc[0:MAIN, :] = zmain[z].astype(F32)
+    acc[MAIN:BLOCK, :] = zrem[...].astype(F32)
+    for i in range(NZ):
+
+        @pl.when(sends(i, z))
+        def _(i=i):
+            zmain_copy(i, z).wait_recv()
+            acc[0:MAIN, :] += zback[i].astype(F32)
+
+    for i in range(NZ):
+
+        @pl.when(sends(i, z))
+        def _(i=i):
+            zrem_copy(i, z).wait_recv()
+            acc[MAIN:BLOCK, :] += zback_rem[i].astype(F32)
+
+    total = acc[0:BLOCK, :]
     rem = total[MAIN:BLOCK]
     one = jnp.sum(jnp.where(row == REM * z, rem, 0.0), axis=0, keepdims=True)
     two = jnp.sum(jnp.where(row == REM * z + 1, rem, 0.0), axis=0, keepdims=True)
@@ -436,27 +467,49 @@
         wcopy(i).wait_recv()
     ecopy().wait_recv()
 
-    def tcopy(d, target):
+    half = cols // 2
+    lo, hi = slice(0, half), slice(half, cols)
+    below, above = y_peer(NY - 1)[1], y_peer(1)[1]
+    targets = (below, above, below, below, above, above)
+    sources = (above, below, above, above, below, below)
+
+    def tcopy(i, target):
         return pltpu.make_async_remote_copy(
-            src_ref=tsend.at[d - 1],
-            dst_ref=trecv.at[d - 1],
-            send_sem=ts.at[d - 1],
-            recv_sem=tr.at[d - 1],
+            src_ref=tsend.at[i],
+            dst_ref=trecv.at[i],
+            send_sem=ts.at[i],
+            recv_sem=tr.at[i],
             device_id={"tp": target},
             device_id_type=MESH,
         )
 
-    for d in order:
-        other, target = y_peer(d)
-        both = (state[d] + dot(etwin[...], wtwin[other], LAST))[0:M]
-        if d:
-            tsend[d - 1] = both.astype(BF16)
-            tcopy(d, target).start()
-    out = both + sg_ref[...].astype(F32)
-    for d in (1, 3, 2):
-        tcopy(d, y_peer(NY - d)[1]).wait_recv()
-        out = out + trecv[d - 1].astype(F32)
-    out_ref[...] = out.astype(BF16)
+    def put(i, value):
+        tsend[i] = value.astype(BF16)
+        tcopy(i, targets[i]).start()
+
+    def take(i):
+        tcopy(i, sources[i]).wait_recv()
+        return trecv[i].astype(F32)
+
+    def both(d):
+        return (state[d] + dot(etwin[...], wtwin[y_peer(d)[0]], LAST))[0:M]
+
+    value = both(2)
+    put(0, value[:, lo])
+    put(1, value[:, hi])
+    value = both(NY - 1)
+    put(3, value[:, hi])
+    state[NY - 1, 0:M, :] = value
+    value = both(1)
+    put(4, value[:, lo])
+    state[1, 0:M, :] = value
+    state[0, 0:M, :] = both(0) + sg_ref[...].astype(F32)
+    put(2, state[NY - 1, 0:M, lo] + take(0))
+    put(5, state[1, 0:M, hi] + take(1))
+    out_hi = state[0, 0:M, hi] + take(3)
+    out_lo = state[0, 0:M, lo] + take(4)
+    out_ref[:, lo] = (out_lo + take(2)).astype(BF16)
+    out_ref[:, hi] = (out_hi + take(5)).astype(BF16)
 
     for copy in stores:
         copy.wait()
@@ -468,17 +521,21 @@
             for copy in zcopies(d, peer, z):
                 copy.wait_send()
 
-        @pl.when(jnp.logical_not(last) | (other < z))
-        def _(d=d, other=other, peer=peer):
-            zback_copy(d, other, peer).wait_send()
+    for i in range(NZ):
+
+        @pl.when(sends(z, i))
+        def _(i=i):
+            zmain_copy(z, i).wait_send()
+            zrem_copy(z, i).wait_send()
 
     lax.fori_loop(1, NX - x, lambda d, c: (xcopy(d, x).wait_send(), c)[1], 0)
-    lax.fori_loop(0, x, lambda g, c: (hop_out(g).wait_send(), c)[1], 0)
+    for piece in range(2):
+        lax.fori_loop(0, x, lambda g, c: (hop_out(g, piece).wait_send(), c)[1], 0)
     for i in range(NY):
         wcopy(i).wait_send()
     ecopy().wait_send()
-    for d in range(1, NY):
-        tcopy(d, y_peer(d)[1]).wait_send()
+    for i in range(len(targets)):
+        tcopy(i, targets[i]).wait_send()
 
 
 def emit_kernel(count, *refs):
@@ -553,14 +610,16 @@
             pltpu.VMEM((NX, GROUP, W2), BF16),
             pltpu.VMEM((NX, GROUP, W2), BF16),
             pltpu.VMEM((GROUP, W2), F32),
-            pltpu.VMEM((NZ, BLOCK, W2), BF16),
-            pltpu.VMEM((NZ - 1, BLOCK, W2), BF16),
+            pltpu.VMEM((NZ, MAIN, W2), BF16),
+            pltpu.VMEM((TILE, W2), BF16),
+            pltpu.VMEM((NZ, MAIN, W2), BF16),
+            pltpu.VMEM((NZ, TILE, W2), BF16),
             pltpu.VMEM((BLOCK, W2), BF16),
             pltpu.VMEM((BLOCK, W2), BF16),
             pltpu.VMEM((NY, cols, W2), BF16),
             pltpu.VMEM((NY, BLOCK, cols), F32),
-            pltpu.VMEM((NY - 1, M, cols), BF16),
-            pltpu.VMEM((NY - 1, M, cols), BF16),
+            pltpu.VMEM((6, M, cols // 2), BF16),
+            pltpu.VMEM((6, M, cols // 2), BF16),
             pltpu.VMEM((TOK, HEADS * HD), BF16),
             pltpu.VMEM((TOK, HD), BF16),
             pltpu.VMEM((TOK, HD), BF16),
@@ -571,12 +630,12 @@
             dma((2, NZ - 1)),
             dma((NX - 1,)),
             dma((NX - 1,)),
-            dma((NX - 1,)),
-            dma((NX,)),
-            dma((NZ - 1,)),
-            dma((NZ - 1,)),
-            dma((NY - 1,)),
-            dma((NY - 1,)),
+            dma((NX - 1, 2)),
+            dma((NX, 2)),
+            dma((2, NZ)),
+            dma((2, NZ)),
+            dma((6,)),
+            dma((6,)),
             dma((NY,)),
             dma((NY,)),
             dma,

time: 59.4 us -> 56.8 us (0.956)
  Pallas kernels: 58.3 us -> 55.6 us
    pallas_call x1, Pallas kernels: 56.3 us -> 53.6 us  [per_device(): pl.pallas_call(layer_kernel, name='layer', out_shape=(jax.ShapeDtypeStruc...]
where the time goes in v5:
time: 56.8 us; the launch traced here: 56.2 us
  Pallas kernels  55.6 us (98%)
  between operations  0.64 us (1%)
    pallas_call x1, Pallas kernels, per_device(): pl.pallas_call(layer_kernel, name='layer', out_shape=(jax.ShapeDtypeStruc...  53.6 us
    pallas_call x1, Pallas kernels, emit(): pl.pallas_call(functools.partial(emit_kernel, count), name='emit', out_sh...  1.97 us

profile of v5, /device:TPU:1, one launch (start us, length us, event | category | flops | bytes accessed | tf_op | source)
XLA Modules:
  0.0 56.2 jit_solution(2662624829544261448)
XLA Ops:
  0.6 53.6 %layer.1 = (bf16[256,1024]{1,0:T(8,128)(2,1)}, bf16[256,128]{1,0:T(8,128)(2,1)}, bf16[256,128]{1,0:T(8,128)(2,1)}, bf16[50,1024]{1,0:T(8,128)(2,1)}) custom-call(bf16[256,1024]{1,0:T(8,128)(2,1)} %q_hbm.1, bf16[256,1024]{1,0:T(8,128)(2,1)} %g_hbm.1, bf16[256,128]{1,0:T(8,128)(2,1)} %ko_hbm.1, bf16[256,128]{1,0:T(8,128)(2,1)} %vo_hbm.1, ...), custom_call_target="tpu_custom_call" | custom-call | tf_op jit(solution)/shard_map/layer/pallas_call | solution.py:576
  54.3 2.0 %emit.1 = (bf16[256,1024]{1,0:T(8,128)(2,1)}, bf16[256,128]{1,0:T(8,128)(2,1)}, bf16[256,128]{1,0:T(8,128)(2,1)}, bf16[50,1024]{1,0:T(8,128)(2,1)}) custom-call(bf16[256,1024]{1,0:T(8,128)(2,1)} %get-tuple-element.8.refs_0_, bf16[256,128]{1,0:T(8,128)(2,1)} %get-tuple-element.9.refs_1_, bf16[256,128]{1,0:T(8,128)(2,1)} %get-tuple-element.10.refs_2_, ...), custom_call_target="tpu_custom_call" | custom-call | tf_op jit(solution)/shard_map/emit/pallas_call | solution.py:558

commit v6 on v5

--- a/solution.py
+++ b/solution.py
@@ -79,7 +79,7 @@
     q_hbm, g_hbm, ko_hbm, vo_hbm, st_hbm, wk_hbm, wv_hbm, sg_hbm,
     dq_hbm, dko_hbm, dvo_hbm, out_ref,
     q_ref, g_ref, ko_ref, vo_ref, st, w, sg_ref,
-    mine, zrecv, grp, s_own, p_own, s_all, p_all, m_ref, l_ref, d_ref, dqt, kt_own, kt,
+    mine, mine_rem, zrecv, grp, s_own, p_own, s_all, p_all, m_ref, l_ref, d_ref, dqt, kt_own, kt,
     dk_acc, dv_acc, part, xback, acc, zmain, zrem, zback, zback_rem, em, etwin, wtwin, state, tsend, trecv, dq_ref, dko_ref, dvo_ref,
     wsem, insem, outsem, zs, zr, xs, xr, xbs, xbr, zbs, zbr, ts, tr, ws, wr, es, er,
 ):
@@ -124,14 +124,9 @@
         wcopies[2 * c + 1].wait()
         chunk = pl.ds(c * rows, rows)
         total = total + dot(st[:, chunk], w[chunk, :])
-    mine[0:MAIN, :] = total[0:MAIN].astype(BF16)
+    mine[...] = total[0:MAIN].astype(BF16)
+    mine_rem[...] = total[MAIN:M].astype(BF16)
     row = lax.broadcasted_iota(jnp.int32, (TILE, W2), 0)
-    shared = jnp.where(
-        row == REM * z,
-        total[MAIN : MAIN + 1],
-        jnp.where(row == REM * z + 1, total[MAIN + 1 : MAIN + 2], 0.0),
-    )
-    mine[MAIN:BLOCK, :] = shared.astype(BF16)
     pl.semaphore_wait(barrier, count)
 
     def rows_of(i):
@@ -141,14 +136,14 @@
         own = {"device_id": {"seg": peer}, "device_id_type": MESH}
         return (
             pltpu.make_async_remote_copy(
-                src_ref=mine.at[0:MAIN],
+                src_ref=mine,
                 dst_ref=grp.at[x, rows_of(slot)],
                 send_sem=zs.at[0, d - 1],
                 recv_sem=zr.at[0, d - 1],
                 **own,
             ),
             pltpu.make_async_remote_copy(
-                src_ref=mine.at[MAIN:BLOCK],
+                src_ref=mine_rem,
                 dst_ref=zrecv.at[slot],
                 send_sem=zs.at[1, d - 1],
                 recv_sem=zr.at[1, d - 1],
@@ -183,11 +178,20 @@
             def _(d=d):
                 xcopy(d, x, part_rows).start()
 
-    grp[x, rows_of(z), :] = mine[0:MAIN, :]
+    grp[x, rows_of(z), :] = mine[...]
     pass_on(rows_of(z))
 
     def assemble(sent_on):
-        acc[0:TILE, :] = mine[MAIN:BLOCK, :].astype(F32)
+        def place_rem(ref, i):
+            two = ref.astype(F32)
+            acc[0:TILE, :] = jnp.where(
+                row == REM * i,
+                two[0:1],
+                jnp.where(row == REM * i + 1, two[1:2], acc[0:TILE, :]),
+            )
+
+        acc[0:TILE, :] = jnp.zeros((TILE, W2), F32)
+        place_rem(mine_rem[...], z)
         for d in near:
             other, peer = z_peer(x, z, NZ - d)
             if sent_on:
@@ -209,7 +213,7 @@
             @pl.when(jnp.bool_(sent_on) | (other < z))
             def _(d=d, other=other, peer=peer):
                 zcopies(d, peer, other)[1].wait_recv()
-                acc[0:TILE, :] += zrecv[other].astype(F32)
+                place_rem(zrecv[other], other)
 
         grp[x, REM0:GROUP, :] = acc[0:TILE, :].astype(BF16)
         if sent_on:
@@ -319,8 +323,7 @@
 
     pieces = (pl.ds(0, HALF), pl.ds(HALF, GROUP - HALF))
 
-    def hop(g, piece, peer_x, wrap):
-        slot = jnp.where(wrap, NX - 1, g)
+    def hop(g, piece, slot, peer_x):
         return pltpu.make_async_remote_copy(
             src_ref=part.at[g, pieces[piece]],
             dst_ref=xback.at[slot, pieces[piece]],
@@ -331,16 +334,18 @@
         )
 
     def hop_out(g, piece):
-        wrap = last & (g == 0)
-        return hop(g, piece, jnp.where(wrap, 0, x - 1), wrap)
-
-    def hop_add(g, piece, peer_x, wrap):
-        hop(g, piece, peer_x, wrap).wait_recv()
+        around = last & ((g == 0) | ((g == 1) & (piece == 1)))
+        slot = jnp.where(around, NX - 1 + g, g)
+        up = (x == 2) & (g == 0)
+        return hop(g, piece, slot, jnp.where(around, 0, jnp.where(up, NX - 1, x - 1)))
+
+    def hop_add(piece, slot, peer_x):
+        hop(0, piece, slot, peer_x).wait_recv()
         rows_in = pieces[piece]
-        acc[rows_in, :] += xback[jnp.where(wrap, NX - 1, g), rows_in, :].astype(F32)
+        acc[rows_in, :] += xback[slot, rows_in, :].astype(F32)
 
     def back_group(i, carry):
-        g = jnp.where(last & (i < 2), 1 - i, i)
+        g = jnp.where(last & (i < x), lax.rem(i + 1, x + (x == 0)), i)
         kt[...] = grp[g, :, 0:HD].astype(F32).T.astype(BF16)
         dk, dv = sweep_two(s_all.at[g], p_all.at[g], kt)
         acc[:, 0:HD] = dk
@@ -350,9 +355,15 @@
         def _():
             for piece in range(2):
 
-                @pl.when((x == 1) | ((x == 2) & (g == 1)))
+                @pl.when(last & (g == 0))
                 def _(piece=piece):
-                    hop_add(g, piece, x + 1, False)
+                    hop_add(piece, 0, 2)
+
+                if piece == 0:
+
+                    @pl.when((x == 2) & (g == 1))
+                    def _():
+                        hop_add(0, 1, NX - 1)
 
                 part[g, pieces[piece], :] = acc[pieces[piece], :].astype(BF16)
                 hop_out(g, piece).start()
@@ -377,7 +388,7 @@
 
     def zrem_copy(source, target):
         return pltpu.make_async_remote_copy(
-            src_ref=zrem,
+            src_ref=zrem.at[target],
             dst_ref=zback_rem.at[source],
             send_sem=zbs.at[1, target],
             recv_sem=zbr.at[1, source],
@@ -388,15 +399,37 @@
     def sends(source, target):
         return (source != target) & (jnp.logical_not(last) | (target < source))
 
+    def relay():
+        return pltpu.make_async_remote_copy(
+            src_ref=xback.at[NX, pieces[1]],
+            dst_ref=xback.at[NX, pieces[1]],
+            send_sem=xbs.at[1, 1],
+            recv_sem=xbr.at[NX, 1],
+            device_id={"seg": NZ + z},
+            device_id_type=MESH,
+        )
+
+    @pl.when(x == 0)
+    def _():
+        hop(1, 1, NX, NX - 1).wait_recv()
+        relay().start()
+
     for piece in range(2):
-
-        @pl.when(jnp.logical_not(last))
-        def _(piece=piece):
-            hop_add(x, piece, x + 1, False)
 
         @pl.when(x == 0)
         def _(piece=piece):
-            hop_add(x, piece, NX - 1, True)
+            hop_add(piece, 0, 1)
+            hop_add(piece, NX - 1, NX - 1)
+
+        @pl.when(x == 1)
+        def _(piece=piece):
+            hop_add(piece, 1, 2)
+            if piece == 1:
+                hop_add(1, NX, 0)
+
+        @pl.when(x == 2)
+        def _(piece=piece):
+            hop_add(piece, 2, NX - 1)
 
         for i in range(piece * NZ // 2, (piece + 1) * NZ // 2):
             zmain[i] = acc[i * MAIN : (i + 1) * MAIN, :].astype(BF16)
@@ -405,8 +438,8 @@
             def _(i=i):
                 zmain_copy(z, i).start()
 
-    zrem[...] = acc[REM0:GROUP, :].astype(BF16)
     for i in range(NZ):
+        zrem[i] = acc[REM0 + REM * i : REM0 + REM * (i + 1), :].astype(BF16)
 
         @pl.when(sends(z, i))
         def _(i=i):
@@ -425,7 +458,7 @@
         copy.start()
 
     acc[0:MAIN, :] = zmain[z].astype(F32)
-    acc[MAIN:BLOCK, :] = zrem[...].astype(F32)
+    acc[MAIN:M, :] = zrem[z].astype(F32)
     for i in range(NZ):
 
         @pl.when(sends(i, z))
@@ -438,14 +471,12 @@
         @pl.when(sends(i, z))
         def _(i=i):
             zrem_copy(i, z).wait_recv()
-            acc[MAIN:BLOCK, :] += zback_rem[i].astype(F32)
-
-    total = acc[0:BLOCK, :]
-    rem = total[MAIN:BLOCK]
-    one = jnp.sum(jnp.where(row == REM * z, rem, 0.0), axis=0, keepdims=True)
-    two = jnp.sum(jnp.where(row == REM * z + 1, rem, 0.0), axis=0, keepdims=True)
-    em[0:MAIN, :] = total[0:MAIN].astype(BF16)
-    em[MAIN:BLOCK, :] = jnp.where(row == 0, one, jnp.where(row == 1, two, 0.0)).astype(BF16)
+            acc[MAIN:M, :] += zback_rem[i].astype(F32)
+
+    em[0:MAIN, :] = acc[0:MAIN, :].astype(BF16)
+    em[MAIN:BLOCK, :] = jnp.where(
+        row == 0, acc[MAIN : MAIN + 1, :], jnp.where(row == 1, acc[MAIN + 1 : M, :], 0.0)
+    ).astype(BF16)
 
     def ecopy():
         return pltpu.make_async_remote_copy(
@@ -534,6 +565,10 @@
     for i in range(NY):
         wcopy(i).wait_send()
     ecopy().wait_send()
+    @pl.when(x == 0)
+    def _():
+        relay().wait_send()
+
     for i in range(len(targets)):
         tcopy(i, targets[i]).wait_send()
 
@@ -592,8 +627,9 @@
             pltpu.VMEM((M, D), BF16),
             pltpu.VMEM((D, W2), BF16),
             pltpu.VMEM((M, cols), BF16),
-            pltpu.VMEM((BLOCK, W2), BF16),
-            pltpu.VMEM((NZ, TILE, W2), BF16),
+            pltpu.VMEM((MAIN, W2), BF16),
+            pltpu.VMEM((REM, W2), BF16),
+            pltpu.VMEM((NZ, REM, W2), BF16),
             pltpu.VMEM((NX, GROUP, W2), BF16),
             pltpu.VMEM((TOK, rows), F32),
             pltpu.VMEM((TOK, rows), F32),
@@ -608,12 +644,12 @@
             pltpu.VMEM((GROUP, HD), F32),
             pltpu.VMEM((GROUP, HD), F32),
             pltpu.VMEM((NX, GROUP, W2), BF16),
-            pltpu.VMEM((NX, GROUP, W2), BF16),
+            pltpu.VMEM((NX + 1, GROUP, W2), BF16),
             pltpu.VMEM((GROUP, W2), F32),
             pltpu.VMEM((NZ, MAIN, W2), BF16),
-            pltpu.VMEM((TILE, W2), BF16),
+            pltpu.VMEM((NZ, REM, W2), BF16),
             pltpu.VMEM((NZ, MAIN, W2), BF16),
-            pltpu.VMEM((NZ, TILE, W2), BF16),
+            pltpu.VMEM((NZ, REM, W2), BF16),
             pltpu.VMEM((BLOCK, W2), BF16),
             pltpu.VMEM((BLOCK, W2), BF16),
             pltpu.VMEM((NY, cols, W2), BF16),
@@ -631,7 +667,7 @@
             dma((NX - 1,)),
             dma((NX - 1,)),
             dma((NX - 1, 2)),
-            dma((NX, 2)),
+            dma((NX + 1, 2)),
             dma((2, NZ)),
             dma((2, NZ)),
             dma((6,)),

time: 56.8 us -> 55 us (0.968)
  Pallas kernels: 55.6 us -> 54.3 us
    pallas_call x1, Pallas kernels: 53.6 us -> 52.3 us  [per_device(): pl.pallas_call(layer_kernel, name='layer', out_shape=(jax.ShapeDtypeStruc...]
where the time goes in v6:
time: 55 us; the launch traced here: 54.9 us
  Pallas kernels  54.3 us (99%)
  between operations  0.64 us (1%)
    pallas_call x1, Pallas kernels, per_device(): pl.pallas_call(layer_kernel, name='layer', out_shape=(jax.ShapeDtypeStruc...  52.3 us
    pallas_call x1, Pallas kernels, emit(): pl.pallas_call(functools.partial(emit_kernel, count), name='emit', out_sh...  1.97 us

profile of v6, /device:TPU:1, one launch (start us, length us, event | category | flops | bytes accessed | tf_op | source)
XLA Modules:
  0.0 54.9 jit_solution(14959799146287653061)
XLA Ops:
  0.6 52.3 %layer.1 = (bf16[256,1024]{1,0:T(8,128)(2,1)}, bf16[256,128]{1,0:T(8,128)(2,1)}, bf16[256,128]{1,0:T(8,128)(2,1)}, bf16[50,1024]{1,0:T(8,128)(2,1)}) custom-call(bf16[256,1024]{1,0:T(8,128)(2,1)} %q_hbm.1, bf16[256,1024]{1,0:T(8,128)(2,1)} %g_hbm.1, bf16[256,128]{1,0:T(8,128)(2,1)} %ko_hbm.1, bf16[256,128]{1,0:T(8,128)(2,1)} %vo_hbm.1, ...), custom_call_target="tpu_custom_call" | custom-call | tf_op jit(solution)/shard_map/layer/pallas_call | solution.py:611
  53.0 2.0 %emit.1 = (bf16[256,1024]{1,0:T(8,128)(2,1)}, bf16[256,128]{1,0:T(8,128)(2,1)}, bf16[256,128]{1,0:T(8,128)(2,1)}, bf16[50,1024]{1,0:T(8,128)(2,1)}) custom-call(bf16[256,1024]{1,0:T(8,128)(2,1)} %get-tuple-element.8.refs_0_, bf16[256,128]{1,0:T(8,128)(2,1)} %get-tuple-element.9.refs_1_, bf16[256,128]{1,0:T(8,128)(2,1)} %get-tuple-element.10.refs_2_, ...), custom_call_target="tpu_custom_call" | custom-call | tf_op jit(solution)/shard_map/emit/pallas_call | solution.py:593

commit v7 on v6

--- a/solution.py
+++ b/solution.py
@@ -299,6 +299,16 @@
     dqt[...] = jnp.zeros_like(dqt)
     sweep_one(ko_ref[...], vo_ref[...], s_own, p_own, tri, True)
 
+    @pl.when(last)
+    def _():
+        assemble(False)
+
+    @pl.when(z > 0)
+    def _():
+        r = lax.broadcasted_iota(jnp.int32, (GROUP, TOK), 0)
+        mask = (r < MAIN * z) | ((r >= REM0) & (r < REM0 + REM * z))
+        sweep_one(grp[x, :, 0:HD], grp[x, :, HD:W2], s_all.at[x], p_all.at[x], mask, False)
+
     def full_group(i, carry):
         d = jnp.where(last & (i > 1), 5 - i, i)
         g = x - d
@@ -307,16 +317,6 @@
         return carry
 
     lax.fori_loop(1, x + 1, full_group, 0)
-
-    @pl.when(last)
-    def _():
-        assemble(False)
-
-    @pl.when(z > 0)
-    def _():
-        r = lax.broadcasted_iota(jnp.int32, (GROUP, TOK), 0)
-        mask = (r < MAIN * z) | ((r >= REM0) & (r < REM0 + REM * z))
-        sweep_one(grp[x, :, 0:HD], grp[x, :, HD:W2], s_all.at[x], p_all.at[x], mask, False)
 
     d_ref[...] = d_ref[...] / l_ref[...]
     m_ref[...] = m_ref[...] + jnp.log2(l_ref[...])

time: 55 us -> 53.2 us (0.967)
  Pallas kernels: 54.3 us -> 52.5 us
    pallas_call x1, Pallas kernels: 52.3 us -> 50.5 us  [per_device(): pl.pallas_call(layer_kernel, name='layer', out_shape=(jax.ShapeDtypeStruc...]
where the time goes in v7:
time: 53.2 us; the launch traced here: 53.1 us
  Pallas kernels  52.5 us (99%)
  between operations  0.64 us (1%)
    pallas_call x1, Pallas kernels, per_device(): pl.pallas_call(layer_kernel, name='layer', out_shape=(jax.ShapeDtypeStruc...  50.5 us
    pallas_call x1, Pallas kernels, emit(): pl.pallas_call(functools.partial(emit_kernel, count), name='emit', out_sh...  1.97 us

profile of v7, /device:TPU:1, one launch (start us, length us, event | category | flops | bytes accessed | tf_op | source)
XLA Modules:
  0.0 53.1 jit_solution(4181867707392197521)
XLA Ops:
  0.6 50.5 %layer.1 = (bf16[256,1024]{1,0:T(8,128)(2,1)}, bf16[256,128]{1,0:T(8,128)(2,1)}, bf16[256,128]{1,0:T(8,128)(2,1)}, bf16[50,1024]{1,0:T(8,128)(2,1)}) custom-call(bf16[256,1024]{1,0:T(8,128)(2,1)} %q_hbm.1, bf16[256,1024]{1,0:T(8,128)(2,1)} %g_hbm.1, bf16[256,128]{1,0:T(8,128)(2,1)} %ko_hbm.1, bf16[256,128]{1,0:T(8,128)(2,1)} %vo_hbm.1, ...), custom_call_target="tpu_custom_call" | custom-call | tf_op jit(solution)/shard_map/layer/pallas_call | solution.py:611
  51.1 2.0 %emit.1 = (bf16[256,1024]{1,0:T(8,128)(2,1)}, bf16[256,128]{1,0:T(8,128)(2,1)}, bf16[256,128]{1,0:T(8,128)(2,1)}, bf16[50,1024]{1,0:T(8,128)(2,1)}) custom-call(bf16[256,1024]{1,0:T(8,128)(2,1)} %get-tuple-element.8.refs_0_, bf16[256,128]{1,0:T(8,128)(2,1)} %get-tuple-element.9.refs_1_, bf16[256,128]{1,0:T(8,128)(2,1)} %get-tuple-element.10.refs_2_, ...), custom_call_target="tpu_custom_call" | custom-call | tf_op jit(solution)/shard_map/emit/pallas_call | solution.py:593

commit v8 on v7

--- a/solution.py
+++ b/solution.py
@@ -21,7 +21,8 @@
 GROUP = NZ * M
 REM0 = NZ * MAIN
 BLOCK = MAIN + TILE
-HALF = REM0 // 2
+PIECES = 4
+PAIR = NZ // PIECES
 D = 8192
 W2 = 2 * HD
 SCALE = HD ** (-0.5)
@@ -321,7 +322,10 @@
     d_ref[...] = d_ref[...] / l_ref[...]
     m_ref[...] = m_ref[...] + jnp.log2(l_ref[...])
 
-    pieces = (pl.ds(0, HALF), pl.ds(HALF, GROUP - HALF))
+    step = PAIR * MAIN
+    pieces = [pl.ds(p * step, step) for p in range(PIECES - 1)]
+    pieces.append(pl.ds((PIECES - 1) * step, GROUP - (PIECES - 1) * step))
+    split = PIECES // 2
 
     def hop(g, piece, slot, peer_x):
         return pltpu.make_async_remote_copy(
@@ -334,7 +338,7 @@
         )
 
     def hop_out(g, piece):
-        around = last & ((g == 0) | ((g == 1) & (piece == 1)))
+        around = last & ((g == 0) | ((g == 1) & (piece >= split)))
         slot = jnp.where(around, NX - 1 + g, g)
         up = (x == 2) & (g == 0)
         return hop(g, piece, slot, jnp.where(around, 0, jnp.where(up, NX - 1, x - 1)))
@@ -353,20 +357,32 @@
 
         @pl.when(g < x)
         def _():
-            for piece in range(2):
+            def put(piece):
+                part[g, pieces[piece], :] = acc[pieces[piece], :].astype(BF16)
+                hop_out(g, piece).start()
+
+            joined = (x == 2) & (g == 1)
+            for piece in range(split, PIECES):
+
+                @pl.when(joined)
+                def _(piece=piece):
+                    put(piece)
+
+            for piece in range(PIECES):
 
                 @pl.when(last & (g == 0))
                 def _(piece=piece):
                     hop_add(piece, 0, 2)
 
-                if piece == 0:
-
-                    @pl.when((x == 2) & (g == 1))
-                    def _():
-                        hop_add(0, 1, NX - 1)
-
-                part[g, pieces[piece], :] = acc[pieces[piece], :].astype(BF16)
-                hop_out(g, piece).start()
+                if piece < split:
+
+                    @pl.when(joined)
+                    def _(piece=piece):
+                        hop_add(piece, 1, NX - 1)
+
+                @pl.when(jnp.logical_not(joined) | (piece < split))
+                def _(piece=piece):
+                    put(piece)
 
         return carry
 
@@ -399,22 +415,23 @@
     def sends(source, target):
         return (source != target) & (jnp.logical_not(last) | (target < source))
 
-    def relay():
+    def relay(piece):
         return pltpu.make_async_remote_copy(
-            src_ref=xback.at[NX, pieces[1]],
-            dst_ref=xback.at[NX, pieces[1]],
-            send_sem=xbs.at[1, 1],
-            recv_sem=xbr.at[NX, 1],
+            src_ref=xback.at[NX, pieces[piece]],
+            dst_ref=xback.at[NX, pieces[piece]],
+            send_sem=xbs.at[1, piece],
+            recv_sem=xbr.at[NX, piece],
             device_id={"seg": NZ + z},
             device_id_type=MESH,
         )
 
     @pl.when(x == 0)
     def _():
-        hop(1, 1, NX, NX - 1).wait_recv()
-        relay().start()
-
-    for piece in range(2):
+        for piece in range(split, PIECES):
+            hop(1, piece, NX, NX - 1).wait_recv()
+            relay(piece).start()
+
+    for piece in range(PIECES):
 
         @pl.when(x == 0)
         def _(piece=piece):
@@ -424,14 +441,14 @@
         @pl.when(x == 1)
         def _(piece=piece):
             hop_add(piece, 1, 2)
-            if piece == 1:
-                hop_add(1, NX, 0)
+            if piece >= split:
+                hop_add(piece, NX, 0)
 
         @pl.when(x == 2)
         def _(piece=piece):
             hop_add(piece, 2, NX - 1)
 
-        for i in range(piece * NZ // 2, (piece + 1) * NZ // 2):
+        for i in range(piece * PAIR, (piece + 1) * PAIR):
             zmain[i] = acc[i * MAIN : (i + 1) * MAIN, :].astype(BF16)
 
             @pl.when(sends(z, i))
@@ -560,14 +577,15 @@
             zrem_copy(z, i).wait_send()
 
     lax.fori_loop(1, NX - x, lambda d, c: (xcopy(d, x).wait_send(), c)[1], 0)
-    for piece in range(2):
+    for piece in range(PIECES):
         lax.fori_loop(0, x, lambda g, c: (hop_out(g, piece).wait_send(), c)[1], 0)
     for i in range(NY):
         wcopy(i).wait_send()
     ecopy().wait_send()
     @pl.when(x == 0)
     def _():
-        relay().wait_send()
+        for piece in range(split, PIECES):
+            relay(piece).wait_send()
 
     for i in range(len(targets)):
         tcopy(i, targets[i]).wait_send()
@@ -666,8 +684,8 @@
             dma((2, NZ - 1)),
             dma((NX - 1,)),
             dma((NX - 1,)),
-            dma((NX - 1, 2)),
-            dma((NX + 1, 2)),
+            dma((NX - 1, PIECES)),
+            dma((NX + 1, PIECES)),
             dma((2, NZ)),
             dma((2, NZ)),
             dma((6,)),

time: 53.2 us -> 53.3 us (level)
  no operation moved by 1% of the time
where the time goes in v8:
time: 53.3 us; the launch traced here: 53.2 us
  Pallas kernels  52.6 us (99%)
  between operations  0.64 us (1%)
    pallas_call x1, Pallas kernels, per_device(): pl.pallas_call(layer_kernel, name='layer', out_shape=(jax.ShapeDtypeStruc...  50.6 us
    pallas_call x1, Pallas kernels, emit(): pl.pallas_call(functools.partial(emit_kernel, count), name='emit', out_sh...  1.97 us

profile of v8, /device:TPU:1, one launch (start us, length us, event | category | flops | bytes accessed | tf_op | source)
XLA Modules:
  0.0 53.2 jit_solution(3115985106282697863)
XLA Ops:
  0.6 50.6 %layer.1 = (bf16[256,1024]{1,0:T(8,128)(2,1)}, bf16[256,128]{1,0:T(8,128)(2,1)}, bf16[256,128]{1,0:T(8,128)(2,1)}, bf16[50,1024]{1,0:T(8,128)(2,1)}) custom-call(bf16[256,1024]{1,0:T(8,128)(2,1)} %q_hbm.1, bf16[256,1024]{1,0:T(8,128)(2,1)} %g_hbm.1, bf16[256,128]{1,0:T(8,128)(2,1)} %ko_hbm.1, bf16[256,128]{1,0:T(8,128)(2,1)} %vo_hbm.1, ...), custom_call_target="tpu_custom_call" | custom-call | tf_op jit(solution)/shard_map/layer/pallas_call | solution.py:629
  51.2 2.0 %emit.1 = (bf16[256,1024]{1,0:T(8,128)(2,1)}, bf16[256,128]{1,0:T(8,128)(2,1)}, bf16[256,128]{1,0:T(8,128)(2,1)}, bf16[50,1024]{1,0:T(8,128)(2,1)}) custom-call(bf16[256,1024]{1,0:T(8,128)(2,1)} %get-tuple-element.8.refs_0_, bf16[256,128]{1,0:T(8,128)(2,1)} %get-tuple-element.9.refs_1_, bf16[256,128]{1,0:T(8,128)(2,1)} %get-tuple-element.10.refs_2_, ...), custom_call_target="tpu_custom_call" | custom-call | tf_op jit(solution)/shard_map/emit/pallas_call | solution.py:611

commit v9 on v8

--- a/solution.py
+++ b/solution.py
@@ -82,7 +82,7 @@
     q_ref, g_ref, ko_ref, vo_ref, st, w, sg_ref,
     mine, mine_rem, zrecv, grp, s_own, p_own, s_all, p_all, m_ref, l_ref, d_ref, dqt, kt_own, kt,
     dk_acc, dv_acc, part, xback, acc, zmain, zrem, zback, zback_rem, em, etwin, wtwin, state, tsend, trecv, dq_ref, dko_ref, dvo_ref,
-    wsem, insem, outsem, zs, zr, xs, xr, xbs, xbr, zbs, zbr, ts, tr, ws, wr, es, er,
+    wsem, insem, outsem, zs, zr, xs, xr, xbs, xbr, zbs, zbr, ts, tr, ws, wr, es, er, gs, gin,
 ):
     x, z = seg_place()
     tp = lax.axis_index("tp")
@@ -173,14 +173,40 @@
             device_id_type=MESH,
         )
 
-    def pass_on(part_rows):
+    near_rows, far_rows = pl.ds(0, REM0 // 2), pl.ds(REM0 // 2, GROUP - REM0 // 2)
+
+    def detour(part_rows, to, send_sem, recv_sem):
+        return pltpu.make_async_remote_copy(
+            src_ref=grp.at[1, part_rows],
+            dst_ref=grp.at[1, part_rows],
+            send_sem=send_sem,
+            recv_sem=recv_sem,
+            device_id={"seg": to * NZ + z},
+            device_id_type=MESH,
+        )
+
+    def pass_on(part_rows, i=NZ):
         for d in (3, 1, 2):
-            @pl.when((x + d < NX) & ((x > 0) | (d != 2)))
+            direct = (x + d < NX) & ((x > 0) | (d != 2))
+            if d == 2:
+                direct = direct & (i >= NZ // 2)
+
+            @pl.when(direct)
             def _(d=d):
                 xcopy(d, x, part_rows).start()
 
+        @pl.when((x == 1) & (i < NZ // 2))
+        def _():
+            detour(part_rows, 0, gs.at[0], gin.at[lax.rem(i, NZ)]).start()
+
+    def turn(i):
+        @pl.when((x == 0) & (i < NZ // 2))
+        def _():
+            detour(rows_of(i), 0, gs.at[0], gin.at[i]).wait_recv()
+            detour(rows_of(i), NX - 1, gs.at[1], gin.at[NZ]).start()
+
     grp[x, rows_of(z), :] = mine[...]
-    pass_on(rows_of(z))
+    pass_on(rows_of(z), z)
 
     def assemble(sent_on):
         def place_rem(ref, i):
@@ -193,11 +219,15 @@
 
         acc[0:TILE, :] = jnp.zeros((TILE, W2), F32)
         place_rem(mine_rem[...], z)
+        passed = [z]
         for d in near:
             other, peer = z_peer(x, z, NZ - d)
             if sent_on:
                 zcopies(d, peer, other)[0].wait_recv()
-                pass_on(rows_of(other))
+                pass_on(rows_of(other), other)
+                passed.append(other)
+                if len(passed) > 2:
+                    turn(passed[-3])
             else:
 
                 @pl.when(other < z)
@@ -219,6 +249,8 @@
         grp[x, REM0:GROUP, :] = acc[0:TILE, :].astype(BF16)
         if sent_on:
             pass_on(pl.ds(REM0, TILE))
+            turn(passed[-2])
+            turn(passed[-1])
 
             @pl.when(x == 0)
             def _():
@@ -313,7 +345,17 @@
     def full_group(i, carry):
         d = jnp.where(last & (i > 1), 5 - i, i)
         g = x - d
-        xcopy(-d, g).wait_recv()
+        parted = last & (g == 1)
+
+        @pl.when(parted)
+        def _():
+            xcopy(-2, g, far_rows).wait_recv()
+            detour(near_rows, 0, gs.at[0], gin.at[NZ]).wait_recv()
+
+        @pl.when(jnp.logical_not(parted))
+        def _():
+            xcopy(-d, g).wait_recv()
+
         sweep_one(grp[g, :, 0:HD], grp[g, :, HD:W2], s_all.at[g], p_all.at[g], None, False)
         return carry
 
@@ -576,7 +618,21 @@
             zmain_copy(z, i).wait_send()
             zrem_copy(z, i).wait_send()
 
-    lax.fori_loop(1, NX - x, lambda d, c: (xcopy(d, x).wait_send(), c)[1], 0)
+    for d in range(1, NX):
+
+        @pl.when((x + d < NX) & ((x != 1) | (d != 2)))
+        def _(d=d):
+            xcopy(d, x).wait_send()
+
+    @pl.when(x == 1)
+    def _():
+        xcopy(2, x, far_rows).wait_send()
+        detour(near_rows, 0, gs.at[0], gin.at[NZ]).wait_send()
+
+    @pl.when(x == 0)
+    def _():
+        detour(near_rows, NX - 1, gs.at[1], gin.at[NZ]).wait_send()
+
     for piece in range(PIECES):
         lax.fori_loop(0, x, lambda g, c: (hop_out(g, piece).wait_send(), c)[1], 0)
     for i in range(NY):
@@ -694,6 +750,8 @@
             dma((NY,)),
             dma,
             dma,
+            dma((2,)),
+            dma((NZ + 1,)),
         ],
         compiler_params=pltpu.CompilerParams(
             collective_id=0, has_side_effects=True, vmem_limit_bytes=58 << 20

time: 53.3 us -> 54.3 us (1.019)
  Pallas kernels: 52.6 us -> 53.6 us
    pallas_call x1, Pallas kernels: 50.6 us -> 51.6 us  [per_device(): pl.pallas_call(layer_kernel, name='layer', out_shape=(jax.ShapeDtypeStruc...]
where the time goes in v9:
time: 54.3 us; the launch traced here: 54.2 us
  Pallas kernels  53.6 us (99%)
  between operations  0.64 us (1%)
    pallas_call x1, Pallas kernels, per_device(): pl.pallas_call(layer_kernel, name='layer', out_shape=(jax.ShapeDtypeStruc...  51.6 us
    pallas_call x1, Pallas kernels, emit(): pl.pallas_call(functools.partial(emit_kernel, count), name='emit', out_sh...  1.97 us

profile of v9, /device:TPU:1, one launch (start us, length us, event | category | flops | bytes accessed | tf_op | source)
XLA Modules:
  0.0 54.2 jit_solution(17547912713288458577)
XLA Ops:
  0.6 51.6 %layer.1 = (bf16[256,1024]{1,0:T(8,128)(2,1)}, bf16[256,128]{1,0:T(8,128)(2,1)}, bf16[256,128]{1,0:T(8,128)(2,1)}, bf16[50,1024]{1,0:T(8,128)(2,1)}) custom-call(bf16[256,1024]{1,0:T(8,128)(2,1)} %q_hbm.1, bf16[256,1024]{1,0:T(8,128)(2,1)} %g_hbm.1, bf16[256,128]{1,0:T(8,128)(2,1)} %ko_hbm.1, bf16[256,128]{1,0:T(8,128)(2,1)} %vo_hbm.1, ...), custom_call_target="tpu_custom_call" | custom-call | tf_op jit(solution)/shard_map/layer/pallas_call | solution.py:685
  52.3 2.0 %emit.1 = (bf16[256,1024]{1,0:T(8,128)(2,1)}, bf16[256,128]{1,0:T(8,128)(2,1)}, bf16[256,128]{1,0:T(8,128)(2,1)}, bf16[50,1024]{1,0:T(8,128)(2,1)}) custom-call(bf16[256,1024]{1,0:T(8,128)(2,1)} %get-tuple-element.8.refs_0_, bf16[256,128]{1,0:T(8,128)(2,1)} %get-tuple-element.9.refs_1_, bf16[256,128]{1,0:T(8,128)(2,1)} %get-tuple-element.10.refs_2_, ...), custom_call_target="tpu_custom_call" | custom-call | tf_op jit(solution)/shard_map/emit/pallas_call | solution.py:667

commit v10 on v8

--- a/solution.py
+++ b/solution.py
@@ -174,7 +174,7 @@
         )
 
     def pass_on(part_rows):
-        for d in (3, 1, 2):
+        for d in (3, 2, 1):
             @pl.when((x + d < NX) & ((x > 0) | (d != 2)))
             def _(d=d):
                 xcopy(d, x, part_rows).start()
@@ -311,7 +311,7 @@
         sweep_one(grp[x, :, 0:HD], grp[x, :, HD:W2], s_all.at[x], p_all.at[x], mask, False)
 
     def full_group(i, carry):
-        d = jnp.where(last & (i > 1), 5 - i, i)
+        d = jnp.where(last, lax.rem(i + 1, NX - 1) + 1, i)
         g = x - d
         xcopy(-d, g).wait_recv()
         sweep_one(grp[g, :, 0:HD], grp[g, :, HD:W2], s_all.at[g], p_all.at[g], None, False)

time: 53.3 us -> 54.2 us (1.017)
  Pallas kernels: 52.6 us -> 53.5 us
    pallas_call x1, Pallas kernels: 50.6 us -> 51.5 us  [per_device(): pl.pallas_call(layer_kernel, name='layer', out_shape=(jax.ShapeDtypeStruc...]
where the time goes in v10:
time: 54.2 us; the launch traced here: 54.1 us
  Pallas kernels  53.5 us (99%)
  between operations  0.64 us (1%)
    pallas_call x1, Pallas kernels, per_device(): pl.pallas_call(layer_kernel, name='layer', out_shape=(jax.ShapeDtypeStruc...  51.5 us
    pallas_call x1, Pallas kernels, emit(): pl.pallas_call(functools.partial(emit_kernel, count), name='emit', out_sh...  1.97 us

profile of v10, /device:TPU:1, one launch (start us, length us, event | category | flops | bytes accessed | tf_op | source)
XLA Modules:
  0.0 54.1 jit_solution(15181669273811270627)
XLA Ops:
  0.6 51.5 %layer.1 = (bf16[256,1024]{1,0:T(8,128)(2,1)}, bf16[256,128]{1,0:T(8,128)(2,1)}, bf16[256,128]{1,0:T(8,128)(2,1)}, bf16[50,1024]{1,0:T(8,128)(2,1)}) custom-call(bf16[256,1024]{1,0:T(8,128)(2,1)} %q_hbm.1, bf16[256,1024]{1,0:T(8,128)(2,1)} %g_hbm.1, bf16[256,128]{1,0:T(8,128)(2,1)} %ko_hbm.1, bf16[256,128]{1,0:T(8,128)(2,1)} %vo_hbm.1, ...), custom_call_target="tpu_custom_call" | custom-call | tf_op jit(solution)/shard_map/layer/pallas_call | solution.py:629
  52.2 2.0 %emit.1 = (bf16[256,1024]{1,0:T(8,128)(2,1)}, bf16[256,128]{1,0:T(8,128)(2,1)}, bf16[256,128]{1,0:T(8,128)(2,1)}, bf16[50,1024]{1,0:T(8,128)(2,1)}) custom-call(bf16[256,1024]{1,0:T(8,128)(2,1)} %get-tuple-element.8.refs_0_, bf16[256,128]{1,0:T(8,128)(2,1)} %get-tuple-element.9.refs_1_, bf16[256,128]{1,0:T(8,128)(2,1)} %get-tuple-element.10.refs_2_, ...), custom_call_target="tpu_custom_call" | custom-call | tf_op jit(solution)/shard_map/emit/pallas_call | solution.py:611

commit v11 on v8

--- a/solution.py
+++ b/solution.py
@@ -241,9 +241,6 @@
             device_id_type=MESH,
         )
 
-    for i in range(NY):
-        wcopy(i).start()
-
     def head(ref, h):
         return ref[:, h * HD : (h + 1) * HD]
 
@@ -387,6 +384,8 @@
         return carry
 
     lax.fori_loop(0, x + jnp.minimum(z, 1), back_group, 0)
+    for i in range(NY):
+        wcopy(i).start()
 
     @pl.when(z == 0)
     def _():

time: 53.3 us -> 53.3 us (level)
  no operation moved by 1% of the time
where the time goes in v11:
time: 53.3 us; the launch traced here: 53.2 us
  Pallas kernels  52.6 us (99%)
  between operations  0.64 us (1%)
    pallas_call x1, Pallas kernels, per_device(): pl.pallas_call(layer_kernel, name='layer', out_shape=(jax.ShapeDtypeStruc...  50.6 us
    pallas_call x1, Pallas kernels, emit(): pl.pallas_call(functools.partial(emit_kernel, count), name='emit', out_sh...  1.97 us

profile of v11, /device:TPU:1, one launch (start us, length us, event | category | flops | bytes accessed | tf_op | source)
XLA Modules:
  0.0 53.2 jit_solution(1429597934123132566)
XLA Ops:
  0.6 50.6 %layer.1 = (bf16[256,1024]{1,0:T(8,128)(2,1)}, bf16[256,128]{1,0:T(8,128)(2,1)}, bf16[256,128]{1,0:T(8,128)(2,1)}, bf16[50,1024]{1,0:T(8,128)(2,1)}) custom-call(bf16[256,1024]{1,0:T(8,128)(2,1)} %q_hbm.1, bf16[256,1024]{1,0:T(8,128)(2,1)} %g_hbm.1, bf16[256,128]{1,0:T(8,128)(2,1)} %ko_hbm.1, bf16[256,128]{1,0:T(8,128)(2,1)} %vo_hbm.1, ...), custom_call_target="tpu_custom_call" | custom-call | tf_op jit(solution)/shard_map/layer/pallas_call | solution.py:628
  51.2 2.0 %emit.1 = (bf16[256,1024]{1,0:T(8,128)(2,1)}, bf16[256,128]{1,0:T(8,128)(2,1)}, bf16[256,128]{1,0:T(8,128)(2,1)}, bf16[50,1024]{1,0:T(8,128)(2,1)}) custom-call(bf16[256,1024]{1,0:T(8,128)(2,1)} %get-tuple-element.8.refs_0_, bf16[256,128]{1,0:T(8,128)(2,1)} %get-tuple-element.9.refs_1_, bf16[256,128]{1,0:T(8,128)(2,1)} %get-tuple-element.10.refs_2_, ...), custom_call_target="tpu_custom_call" | custom-call | tf_op jit(solution)/shard_map/emit/pallas_call | solution.py:610

commit v12 on v7

--- a/solution.py
+++ b/solution.py
@@ -310,7 +310,7 @@
         sweep_one(grp[x, :, 0:HD], grp[x, :, HD:W2], s_all.at[x], p_all.at[x], mask, False)
 
     def full_group(i, carry):
-        d = jnp.where(last & (i > 1), 5 - i, i)
+        d = jnp.where(last, lax.rem(i + 1, NX - 1) + 1, i)
         g = x - d
         xcopy(-d, g).wait_recv()
         sweep_one(grp[g, :, 0:HD], grp[g, :, HD:W2], s_all.at[g], p_all.at[g], None, False)

time: 53.2 us -> 54.7 us (1.028)
  Pallas kernels: 52.5 us -> 54 us
    pallas_call x1, Pallas kernels: 50.5 us -> 52 us  [per_device(): pl.pallas_call(layer_kernel, name='layer', out_shape=(jax.ShapeDtypeStruc...]
where the time goes in v12:
time: 54.7 us; the launch traced here: 54.6 us
  Pallas kernels  54 us (99%)
  between operations  0.64 us (1%)
    pallas_call x1, Pallas kernels, per_device(): pl.pallas_call(layer_kernel, name='layer', out_shape=(jax.ShapeDtypeStruc...  52 us
    pallas_call x1, Pallas kernels, emit(): pl.pallas_call(functools.partial(emit_kernel, count), name='emit', out_sh...  1.97 us

profile of v12, /device:TPU:1, one launch (start us, length us, event | category | flops | bytes accessed | tf_op | source)
XLA Modules:
  0.0 54.6 jit_solution(11364864346272353987)
XLA Ops:
  0.6 52.0 %layer.1 = (bf16[256,1024]{1,0:T(8,128)(2,1)}, bf16[256,128]{1,0:T(8,128)(2,1)}, bf16[256,128]{1,0:T(8,128)(2,1)}, bf16[50,1024]{1,0:T(8,128)(2,1)}) custom-call(bf16[256,1024]{1,0:T(8,128)(2,1)} %q_hbm.1, bf16[256,1024]{1,0:T(8,128)(2,1)} %g_hbm.1, bf16[256,128]{1,0:T(8,128)(2,1)} %ko_hbm.1, bf16[256,128]{1,0:T(8,128)(2,1)} %vo_hbm.1, ...), custom_call_target="tpu_custom_call" | custom-call | tf_op jit(solution)/shard_map/layer/pallas_call | solution.py:611
  52.7 2.0 %emit.1 = (bf16[256,1024]{1,0:T(8,128)(2,1)}, bf16[256,128]{1,0:T(8,128)(2,1)}, bf16[256,128]{1,0:T(8,128)(2,1)}, bf16[50,1024]{1,0:T(8,128)(2,1)}) custom-call(bf16[256,1024]{1,0:T(8,128)(2,1)} %get-tuple-element.8.refs_0_, bf16[256,128]{1,0:T(8,128)(2,1)} %get-tuple-element.9.refs_1_, bf16[256,128]{1,0:T(8,128)(2,1)} %get-tuple-element.10.refs_2_, ...), custom_call_target="tpu_custom_call" | custom-call | tf_op jit(solution)/shard_map/emit/pallas_call | solution.py:593
